TPU v7x, 512 devices: a whole 4x8x8 slice. The times are simulated.
512 devices in a mesh: pipe: 64 (over y, x, core), fsdp: 4 (over z_lo), dp: 2 (over z_hi).
Axes of the slice: x: 4, y: 8, z: 8 (z_hi: 2, z_lo: 4; z = z_hi * 4 + z_lo), core: 2. Of those that a mesh axis runs over, the one named last changes fastest.
Arguments:
- acts: bfloat16 [64, 4, 256, 8192], P('pipe', None, ('fsdp', 'dp')), may hold values from -130 to 130
- cotangent: bfloat16 [64, 4, 256, 512], P('pipe', None, ('fsdp', 'dp')), may hold values from -0.1796875 to 0.1796875
- order: int32 [64, 8, 4], P('pipe', ('fsdp', 'dp')), may hold values from 0 to 3, each once within a row
- key_weight: bfloat16 [64, 8192, 512], P('pipe', 'fsdp'), may hold values from -0.0625 to 0.0625
- gain: float32 [64, 8192], P('pipe', 'fsdp'), may hold values from 0.1 to 1.9
Outputs:
- weight_grad: bfloat16 [64, 8192, 256], P('pipe', ('fsdp', 'dp'))
- gain_grad: float32 [64, 8192], P('pipe', 'fsdp')
Inputs may be any that keep to these rules, and one draw needn't show every extreme that they name: Each row of order is a permutation of 0 to 3.
All inputs are finite; a program needn't handle non-finite values.
Results may differ from a plain program's by a relative error of at most 0.0057.
Values may be sent and summed in bfloat16 or wider, within the bound.
No kernel may reach another device: no remote copies, remote signals or barrier semaphores. Data moves between devices by JAX's collectives and lax.ppermute only.
A program may use at most 128 MiB of HBM per device.

v0:
```python
import jax
import jax.numpy as jnp
from jax import lax
from jax.sharding import PartitionSpec as P


def from_behind(block, axis, distance):
    devices = range(lax.axis_size(axis))
    route = [((i - distance) % len(devices), i) for i in devices]
    return lax.ppermute(block, axis, route)


def local(acts, cotangent, order, key_weight, gain):
    inputs = acts[0]
    batches, tok_rows, width = inputs.shape
    key_width = cotangent.shape[-1]
    floats = inputs.astype(jnp.float32)
    rstd = lax.rsqrt(jnp.mean(floats * floats, axis=-1, keepdims=True) + 1e-05)
    normed = (floats * rstd).astype(jnp.bfloat16)
    onehot = (order[0, 0][:, None] == jnp.arange(batches, dtype=jnp.int32)[None, :]).astype(
        jnp.float32
    )
    key_grad = jnp.einsum("jm,jtk->mtk", onehot, cotangent[0].astype(jnp.float32)).astype(
        jnp.bfloat16
    )
    groups = lax.axis_size(("fsdp", "dp"))
    feat_rows = width // groups
    replica = lax.axis_index("dp")
    received = lax.all_to_all(normed, ("fsdp", "dp"), split_axis=2, concat_axis=1, tiled=True)
    gain_local = gain[0]
    gain_slab = lax.dynamic_slice_in_dim(gain_local, replica * feat_rows, feat_rows, 0)
    scaled = (received.astype(jnp.float32) * gain_slab).astype(jnp.bfloat16)
    weight_local = key_weight[0]
    flat_grad = key_grad.reshape(batches * tok_rows, key_width)
    flat_normed = normed.reshape(batches * tok_rows, width)
    product = jnp.einsum(
        "tk,dk->td",
        flat_grad,
        lax.all_gather(weight_local, "fsdp", axis=0, tiled=True),
        preferred_element_type=jnp.float32,
    )
    gain_terms = jnp.sum(product * flat_normed.astype(jnp.float32), axis=0)
    gain_total = lax.psum(gain_terms, ("fsdp", "dp"))
    shard_len = gain_local.shape[0]
    own_gain = lax.dynamic_slice_in_dim(
        gain_total, lax.axis_index("fsdp") * shard_len, shard_len, 0
    )
    local_w = jnp.einsum(
        "mtd,mtk->dk",
        scaled,
        lax.all_gather(key_grad, ("fsdp", "dp"), axis=1, tiled=True),
        preferred_element_type=jnp.float32,
    )
    half_width = key_width // 2
    ranks = lax.axis_size("pipe")
    middle = ranks // 2
    upper = (lax.axis_index("pipe") >= middle).astype(jnp.int32)
    keeping = lax.dynamic_slice_in_dim(local_w, upper * half_width, half_width, 1)
    sending = lax.dynamic_slice_in_dim(local_w, (1 - upper) * half_width, half_width, 1)
    arrived_w, arrived_g = from_behind((sending, own_gain), "pipe", middle)
    weight_out = (keeping + arrived_w).astype(jnp.bfloat16)
    gain_pair = own_gain + arrived_g
    return (weight_out[None], gain_pair[None])


def solution(mesh):
    return jax.shard_map(
        local,
        mesh=mesh,
        in_specs=(
            P("pipe", None, ("fsdp", "dp"), None),
            P("pipe", None, ("fsdp", "dp"), None),
            P("pipe", ("fsdp", "dp"), None),
            P("pipe", "fsdp", None),
            P("pipe", "fsdp"),
        ),
        out_specs=(P("pipe", ("fsdp", "dp"), None), P("pipe", "fsdp")),
        check_vma=False,
    )
```

profile of v0, /device:TPU:2, one launch (start us, length us, event | category | flops | bytes accessed | tf_op | source)
XLA Modules:
  0.0 339.9 jit_solution(2991144847124069973)
XLA Ops:
  7.2 0.8 copy-done
  8.1 1.5 convolution_convert_fusion
  9.7 0.7 all-gather.6.cloned.1.call-update
  10.4 2.1 fusion.3
  12.5 1.8 fusion.4
  14.3 10.8 %copy.27 = bf16[4,32,8192]{1,0,2:T(4,128)(2,1)} copy(bf16[4,32,8192]{2,1,0:T(8,128)(2,1)} %fusion.4) | data formatting | bytes 4194304 | tf_op jit(solution)/shard_map/convert_element_type | solution.py:19
  25.1 11.2 %reshape.45 = bf16[8,2,65536]{2,1,0:T(2,128)(2,1)} reshape(bf16[8192,4,32]{2,1,0:T(4,128)(2,1)} %bitcast.46) | data formatting | bytes 4194304
  36.3 10.4 %all-to-all-start = ((bf16[8,2,65536]{2,1,0:T(2,128)(2,1)}), bf16[8,2,65536]{2,1,0:T(2,128)(2,1)}, u32[]{:S(2)}, u32[]{:S(2)}) async-start(bf16[8,2,65536]{2,1,0:T(2,128)(2,1)} %reshape.45), calls=%async_computation | async-start | bytes 4194304 | tf_op jit(solution)/shard_map/all_to_all | solution.py:29
  46.8 65.7 %all-to-all-done = bf16[8,2,65536]{2,1,0:T(2,128)(2,1)} async-done(((bf16[8,2,65536]{2,1,0:T(2,128)(2,1)}), bf16[8,2,65536]{2,1,0:T(2,128)(2,1)}, u32[]{:S(2)}, u32[]{:S(2)}) %all-to-all-start) | async-done | bytes 2097184 | tf_op jit(solution)/shard_map/all_to_all | solution.py:29
  112.6 8.7 %reshape.46 = bf16[8192,4,32]{2,1,0:T(4,128)(2,1)} reshape(bf16[8,2,65536]{2,1,0:T(2,128)(2,1)} %all-to-all-done) | data formatting | bytes 4194304
  121.3 10.9 %copy.28 = bf16[4,32,8192]{2,1,0:T(8,128)(2,1)} copy(bf16[4,32,8192]{1,0,2:T(4,128)(2,1)} %bitcast.47) | data formatting | bytes 4194304 | tf_op jit(solution)/shard_map/all_to_all | solution.py:29
  132.1 3.6 %copy.35 = f32[16,8,8,1024]{3,2,1,0:T(8,128)S(1)} copy(bf16[16,8,8,1024]{3,1,2,0:T(8,128)(2,1)} %bitcast.49) | data formatting | bytes 6291456
  136.3 2.4 copy.29
  138.7 2.0 fusion.2
  140.7 3.2 convolution_bitcast_fusion
  143.9 1.3 copy-done.2
  145.3 7.5 %collective-permute-start = (f32[1024,256]{1,0:T(8,128)S(1)}, f32[1024,256]{1,0:T(8,128)}, u32[]{:S(2)}, u32[]{:S(2)}) collective-permute-start(f32[1024,256]{1,0:T(8,128)S(1)} %constant_dynamic-slice_fusion), channel_id=1, source_target_pairs={{256,0},{264,8},{272,16},{280,24},{288,32},{296,40},{304,48},{312,... | collective-permute-start | bytes 3145736 | tf_op jit(solution)/shard_map/ppermute | solution.py:10
  152.8 1.8 fusion.1
  154.6 120.1 %all-gather.6.cloned.1.call-done = bf16[1,8192,512]{2,1,0:T(8,128)(2,1)} async-done(((bf16[1,2048,512]{2,1,0:T(8,128)(2,1)}), bf16[1,8192,512]{2,1,0:T(8,128)(2,1)}) %all-gather.6.cloned.1.call-update) | async-done | bytes 8388624 | tf_op jit(solution)/shard_map/all_gather | solution.py:39
  274.7 7.0 %fusion.5 = f32[8192]{0:T(1024)S(1)} fusion(bf16[128,8192]{1,0:T(8,128)(2,1)} %fusion.1, bf16[128,512]{1,0:T(8,128)(2,1)S(1)} %bitcast.50, bf16[1,8192,512]{2,1,0:T(8,128)(2,1)} %all-gather.6.cloned.1.call-done), kind=kOutput, calls=%fused_computation.11 | convolution fusion | flops 1076879360 | bytes 10649600 | tf_op jit(solution)/shard_map/tk,dk->td/dot_general | solution.py:36
  281.7 41.2 %psum.7 = f32[8192]{0:T(1024)S(1)} all-reduce(f32[8192]{0:T(1024)S(1)} %fusion.5), channel_id=1, replica_groups=mesh['pipe'=64,'fsdp'=4,'dp'=2] {'fsdp','dp'}, use_global_device_ids=true, to_apply=%region_2.0 | all-reduce | flops 8192 | bytes 65536 | tf_op jit(solution)/shard_map/psum | solution.py:43
  322.9 7.3 %collective-permute-start.1 = (f32[2048]{0:T(1024)S(1)}, f32[2048]{0:T(1024)S(1)}, u32[]{:S(2)}, u32[]{:S(2)}) collective-permute-start(f32[2048]{0:T(1024)S(1)} %dynamic_slice.15), channel_id=1, source_target_pairs={{256,0},{264,8},{272,16},{280,24},{288,32},{296,40},{304,48},{312,... | collective-permute-start | bytes 24584 | tf_op jit(solution)/shard_map/ppermute | solution.py:10
  330.3 2.2 fusion.9
  332.5 0.6 dynamic-slice_add_fusion
  (23 shorter events, 0.9 us)
Async XLA Ops:
  7.2 0.9 copy-start
  7.2 5.3 %copy-start.1 = (bf16[1,4,32,8192]{3,2,1,0:T(8,128)(2,1)S(1)}, bf16[1,4,32,8192]{3,2,1,0:T(8,128)(2,1)}, u32[]{:S(2)}) copy-start(bf16[1,4,32,8192]{3,2,1,0:T(8,128)(2,1)} %param.5) | copy-start | bytes 6291460
  7.2 133.5 %all-gather.4.cloned.1.call-start = ((), (), s32[]{:S(2)}) async-start(), calls=%async_computation.1 | async-start | bytes 1179648 | tf_op jit(solution)/shard_map/all_gather | solution.py:51
  9.6 265.1 %all-gather.6.cloned.1.call-start = ((), (), s32[]{:S(2)}) async-start(), calls=%async_computation.2 | async-start | bytes 10485760 | tf_op jit(solution)/shard_map/all_gather | solution.py:39
  36.3 10.5 %copy-start.5 = (f32[1,2048]{1,0:T(1,128)S(1)}, f32[1,2048]{1,0:T(1,128)}, u32[]{:S(2)}) copy-start(f32[1,2048]{1,0:T(1,128)} %param.9) | copy-start | bytes 24580
  36.3 76.2 %all-to-all-start = ((bf16[8,2,65536]{2,1,0:T(2,128)(2,1)}), bf16[8,2,65536]{2,1,0:T(2,128)(2,1)}, u32[]{:S(2)}, u32[]{:S(2)}) async-start(bf16[8,2,65536]{2,1,0:T(2,128)(2,1)} %reshape.45), calls=%async_computation | async-start | bytes 4194304 | tf_op jit(solution)/shard_map/all_to_all | solution.py:29
  143.9 1.4 copy-start.2
  145.2 9.4 %copy-start.4 = (bf16[4,32,512]{2,0,1:T(4,128)(2,1)S(1)}, bf16[4,32,512]{2,0,1:T(4,128)(2,1)}, u32[]{:S(2)}) copy-start(bf16[4,32,512]{2,0,1:T(4,128)(2,1)} %convolution_convert_fusion) | copy-start | bytes 393220
  145.3 185.0 %collective-permute-start = (f32[1024,256]{1,0:T(8,128)S(1)}, f32[1024,256]{1,0:T(8,128)}, u32[]{:S(2)}, u32[]{:S(2)}) collective-permute-start(f32[1024,256]{1,0:T(8,128)S(1)} %constant_dynamic-slice_fusion), channel_id=1, source_target_pairs={{256,0},{264,8},{272,16},{280,24},{288,32},{296,40},{304,48},{312,... | collective-permute-start | bytes 3145736 | tf_op jit(solution)/shard_map/ppermute | solution.py:10
  274.7 55.5 %copy-start.3 = (f32[1024,512]{1,0:T(8,128)S(1)}, f32[1024,512]{1,0:T(8,128)}, u32[]{:S(2)}) copy-start(f32[1024,512]{1,0:T(8,128)} %copy-done.2) | copy-start | bytes 6291460
  322.9 9.5 %collective-permute-start.1 = (f32[2048]{0:T(1024)S(1)}, f32[2048]{0:T(1024)S(1)}, u32[]{:S(2)}, u32[]{:S(2)}) collective-permute-start(f32[2048]{0:T(1024)S(1)} %dynamic_slice.15), channel_id=1, source_target_pairs={{256,0},{264,8},{272,16},{280,24},{288,32},{296,40},{304,48},{312,... | collective-permute-start | bytes 24584 | tf_op jit(solution)/shard_map/ppermute | solution.py:10
Sparse Core Ops, SparseCore 0:
  10.7 102.4 all-gather.3
  115.3 159.4 all-gather.5
where the time goes:
time: 341 us; the launch traced here: 340 us
  waiting for transfers between devices  187 us (55%)
  local copies, waits for them, and re-layouts  50.6 us (15%)
  blocking collectives  41.2 us (12%)
  starting transfers between devices  25.3 us (7%)
  between operations  14.1 us (4%)
  matrix products  11.7 us (3%)
  other arithmetic  10.4 us (3%)
    all_gather x1, waiting for transfers between devices, local(): lax.all_gather(weight_local, 'fsdp', axis=0, tiled=True)  120 us
    all_to_all x1, waiting for transfers between devices, local(): lax.all_to_all(normed, ('fsdp', 'dp'), split_axis=2, concat_axis=1, tiled...  65.7 us
    psum x1, blocking collectives, local(): gain_total = lax.psum(gain_terms, ('fsdp', 'dp'))  41.2 us
    unnamed x15, local copies, waits for them, and re-layouts  25.7 us
    ppermute x2, starting transfers between devices, from_behind(): return lax.ppermute(block, axis, route)  14.8 us
    all_to_all x1, local copies, waits for them, and re-layouts, local(): lax.all_to_all(normed, ('fsdp', 'dp'), split_axis=2, concat_axis=1, tiled...  10.9 us
    convert_element_type x1, local copies, waits for them, and re-layouts, local(): normed = (floats * rstd).astype(jnp.bfloat16)  10.8 us
    all_to_all x1, starting transfers between devices, local(): lax.all_to_all(normed, ('fsdp', 'dp'), split_axis=2, concat_axis=1, tiled...  10.4 us
  transfers between devices with their start and end apart: 5, of which 2 were waited for; matrix products, arithmetic and copies ran while one was open for 20% of the time, Pallas kernels for 0%

commit v1 on v0

v1 whole, which is shorter than its diff:
```python
import functools

import jax
import jax.numpy as jnp
from jax import lax
from jax.experimental import pallas as pl
from jax.experimental.pallas import tpu as pltpu
from jax.sharding import PartitionSpec as P

GROUP = ("fsdp", "dp")
CHUNKS = (1024,)
EPS = 1e-05


def split_kernel(groups, chunks, order_ref, acts_ref, cot_ref, first_ref, *rest_refs):
    del order_ref
    width = acts_ref.shape[-1]
    slab = width // groups
    tokens = acts_ref.shape[-2]
    squares = jnp.zeros((tokens, 128), jnp.float32)
    keys = cot_ref.shape[-1]
    for q in range(groups):
        start = q * slab
        for i, rows in enumerate(chunks):
            part = acts_ref[0, 0, :, start : start + rows]
            if i == 0:
                first_ref[q, :, keys:] = part
            else:
                rest_refs[i - 1][q] = part
            floats = part.astype(jnp.float32)
            floats = floats * floats
            for c in range(0, rows, 128):
                squares += floats[:, c : c + 128]
            start += rows
    rstd = lax.rsqrt(jnp.sum(squares, axis=-1, keepdims=True) / width + EPS)
    grads = (cot_ref[0, 0].astype(jnp.float32) * rstd).astype(jnp.bfloat16)
    for q in range(groups):
        first_ref[q, :, :keys] = grads


def split(acts, cotangent, order, groups, chunks):
    _, batches, tokens, width = acts.shape
    keys = cotangent.shape[-1]

    def slot(m, order_ref):
        found = jnp.int32(0)
        for j in range(1, batches):
            found = jnp.where(order_ref[j] == m, jnp.int32(j), found)
        return (0, found, 0, 0)

    sizes = (keys + chunks[0],) + tuple(chunks[1:])
    return pl.pallas_call(
        functools.partial(split_kernel, groups, chunks),
        out_shape=tuple(
            jax.ShapeDtypeStruct((groups, batches * tokens, n), jnp.bfloat16) for n in sizes
        ),
        grid_spec=pltpu.PrefetchScalarGridSpec(
            num_scalar_prefetch=1,
            grid=(batches,),
            in_specs=[
                pl.BlockSpec((1, 1, tokens, width), lambda m, o: (0, m, 0, 0)),
                pl.BlockSpec((1, 1, tokens, keys), slot),
            ],
            out_specs=tuple(
                pl.BlockSpec((groups, tokens, n), lambda m, o: (0, m, 0)) for n in sizes
            ),
        ),
        cost_estimate=pl.CostEstimate(flops=1 << 21, bytes_accessed=5 << 20, transcendentals=128),
        name="split",
    )(order.reshape(-1), acts, cotangent)


def product_kernel(upper_ref, at_ref, acts_ref, grads_ref, weight_ref, gain_ref, keep_ref, send_ref, gterm_ref):
    del at_ref
    total = lax.dot_general(
        acts_ref[...], grads_ref[...], (((0,), (0,)), ((), ())), preferred_element_type=jnp.float32
    )
    rows, keys = total.shape
    terms = total * weight_ref[0].astype(jnp.float32)
    folded = terms[:, :128]
    for c in range(128, keys, 128):
        folded += terms[:, c : c + 128]
    gterm_ref[...] = jnp.sum(folded.T, axis=0, keepdims=True)
    scaled = total * gain_ref[0].reshape(rows, 1)
    half = keys // 2

    @pl.when(upper_ref[0] == 0)
    def _():
        keep_ref[...] = scaled[:, :half]
        send_ref[...] = scaled[:, half:].astype(jnp.bfloat16)

    @pl.when(upper_ref[0] != 0)
    def _():
        keep_ref[...] = scaled[:, half:]
        send_ref[...] = scaled[:, :half].astype(jnp.bfloat16)


def product(upper, replica, acts, skip, grads_from, weight, gain, offset, rows, slab):
    tokens = acts.shape[0]
    keys = weight.shape[-1]
    tile = 256
    first = (replica * slab + offset) // tile
    return pl.pallas_call(
        product_kernel,
        out_shape=(
            jax.ShapeDtypeStruct((rows, keys // 2), jnp.float32),
            jax.ShapeDtypeStruct((rows, keys // 2), jnp.bfloat16),
            jax.ShapeDtypeStruct((1, rows), jnp.float32),
        ),
        grid_spec=pltpu.PrefetchScalarGridSpec(
            num_scalar_prefetch=2,
            grid=(rows // tile,),
            in_specs=[
                pl.BlockSpec((tokens, tile), lambda i, u, a: (0, skip // tile + i)),
                pl.BlockSpec((tokens, keys), lambda i, u, a: (0, 0)),
                pl.BlockSpec((1, tile, keys), lambda i, u, a: (0, a[0] + i, 0)),
                pl.BlockSpec((1, tile), lambda i, u, a: (0, a[0] + i)),
            ],
            out_specs=(
                pl.BlockSpec((tile, keys // 2), lambda i, u, a: (i, 0)),
                pl.BlockSpec((tile, keys // 2), lambda i, u, a: (i, 0)),
                pl.BlockSpec((1, tile), lambda i, u, a: (0, i)),
            ),
        ),
        cost_estimate=pl.CostEstimate(
            flops=2 * tokens * rows * keys,
            bytes_accessed=2 * tokens * (rows + keys) + 4 * rows * keys,
            transcendentals=0,
        ),
        name="product",
    )(upper, first.reshape(1), acts, grads_from, weight, gain)


def local(acts, cotangent, order, key_weight, gain):
    groups = lax.axis_size(GROUP)
    width = acts.shape[-1]
    slab = width // groups
    keys = cotangent.shape[-1]
    tokens = acts.shape[1] * acts.shape[2]
    ranks = lax.axis_size("pipe")
    middle = ranks // 2
    upper = (lax.axis_index("pipe") >= middle).astype(jnp.int32).reshape(1)
    replica = lax.axis_index("dp")
    across = [(i, (i + middle) % ranks) for i in range(ranks)]
    copies = lax.axis_size("dp")
    beside = [(i, (i + 1) % copies) for i in range(copies)]

    sent = split(acts, cotangent, order, groups, CHUNKS)
    got = [lax.all_to_all(block, GROUP, 0, 0, tiled=True) for block in sent]
    got = [block.reshape(groups * tokens, block.shape[-1]) for block in got]
    offset = 0
    kept, arrived, gterms = [], [], []
    for i, (block, rows) in enumerate(zip(got, CHUNKS)):
        skip = keys if i == 0 else 0
        keep, send, gterm = product(
            upper, replica, block, skip, got[0], key_weight, gain, offset, rows, slab
        )
        kept.append(keep)
        arrived.append(lax.ppermute(send, "pipe", across))
        gterms.append(gterm)
        offset += rows
    gown = jnp.concatenate(gterms, axis=1)
    gpair = gown + lax.ppermute(gown, "pipe", across)
    gbeside = lax.ppermute(gpair, "dp", beside)
    gain_pair = jnp.where(
        replica == 0,
        jnp.concatenate([gpair, gbeside], axis=1),
        jnp.concatenate([gbeside, gpair], axis=1),
    )
    weight_out = jnp.concatenate(
        [(keep + block).astype(jnp.bfloat16) for keep, block in zip(kept, arrived)], axis=0
    )
    return (weight_out[None], gain_pair)


def solution(mesh):
    return jax.shard_map(
        local,
        mesh=mesh,
        in_specs=(
            P("pipe", None, GROUP, None),
            P("pipe", None, GROUP, None),
            P("pipe", GROUP, None),
            P("pipe", "fsdp", None),
            P("pipe", "fsdp"),
        ),
        out_specs=(P("pipe", GROUP, None), P("pipe", "fsdp")),
        check_vma=False,
    )
```

time: 341 us -> 138 us (0.40)
  the two profiles are of different devices: /device:TPU:2 before, /device:TPU:146 now
where the time goes in v1:
time: 138 us; the launch traced here: 137 us
  waiting for transfers between devices  100 us (72%)
  starting transfers between devices  20.7 us (15%)
  Pallas kernels  10.5 us (8%)
  other arithmetic  3.43 us (2%)
  local copies, waits for them, and re-layouts  1.65 us (1%)
    all_to_all x1, waiting for transfers between devices, local(): got = [lax.all_to_all(block, GROUP, 0, 0, tiled=True) for block in sent]  71.4 us
    ppermute x1, waiting for transfers between devices, local(): gpair = gown + lax.ppermute(gown, 'pipe', across)  21.3 us
    all_to_all x1, starting transfers between devices, local(): got = [lax.all_to_all(block, GROUP, 0, 0, tiled=True) for block in sent]  9.06 us
    ppermute x1, waiting for transfers between devices, local(): gbeside = lax.ppermute(gpair, 'dp', beside)  7.48 us
    ppermute x1, starting transfers between devices, local(): arrived.append(lax.ppermute(send, 'pipe', across))  5.96 us
    pallas_call x1, Pallas kernels, product(): pl.pallas_call(product_kernel, out_shape=(jax.ShapeDtypeStruct((rows, key...  5.41 us
    pallas_call x1, Pallas kernels, split(): pl.pallas_call(functools.partial(split_kernel, groups, chunks), out_shape...  5.09 us
    ppermute x1, starting transfers between devices, local(): gpair = gown + lax.ppermute(gown, 'pipe', across)  3.77 us
  transfers between devices with their start and end apart: 4, of which 3 were waited for; matrix products, arithmetic and copies ran while one was open for 1% of the time, Pallas kernels for 0%

profile of v1, /device:TPU:146, one launch (start us, length us, event | category | flops | bytes accessed | tf_op | source)
XLA Modules:
  0.0 137.1 jit_solution(3103364490745745364)
XLA Ops:
  0.6 5.1 %split.1 = bf16[8,128,1536]{2,1,0:T(8,128)(2,1)} custom-call(s32[4]{0:T(128)} %bitcast.8, bf16[1,4,32,8192]{3,2,1,0:T(8,128)(2,1)} %acts_ref.1, bf16[1,4,32,512]{3,2,1,0:T(8,128)(2,1)} %cot_ref.1), custom_call_target="tpu_custom_call" | custom-call | flops 2097152 | bytes 5242880 | tf_op jit(solution)/shard_map/split/pallas_call | solution.py:52
  5.7 9.1 %all-to-all-start = ((bf16[8,128,1536]{2,1,0:T(8,128)(2,1)}), bf16[8,128,1536]{2,1,0:T(8,128)(2,1)S(1)}, u32[]{:S(2)}, u32[]{:S(2)}) async-start(bf16[8,128,1536]{2,1,0:T(8,128)(2,1)} %split.1), calls=%async_computation | async-start | bytes 6291456 | tf_op jit(solution)/shard_map/all_to_all | solution.py:149
  14.8 71.4 %all-to-all-done = bf16[8,128,1536]{2,1,0:T(8,128)(2,1)S(1)} async-done(((bf16[8,128,1536]{2,1,0:T(8,128)(2,1)}), bf16[8,128,1536]{2,1,0:T(8,128)(2,1)S(1)}, u32[]{:S(2)}, u32[]{:S(2)}) %all-to-all-start) | async-done | bytes 3145760 | tf_op jit(solution)/shard_map/all_to_all | solution.py:149
  86.1 0.0 copy-start
  86.1 1.6 %copy-done = bf16[8,128,1536]{2,1,0:T(8,128)(2,1)} copy-done((bf16[8,128,1536]{2,1,0:T(8,128)(2,1)}, bf16[8,128,1536]{2,1,0:T(8,128)(2,1)S(1)}, u32[]{:S(2)}) %copy-start) | copy-done | bytes 3145752
  87.8 5.4 %product.1 = (f32[1024,256]{1,0:T(8,128)}, bf16[1024,256]{1,0:T(8,128)(2,1)}, f32[1,1024]{1,0:T(1,128)}) custom-call(s32[1]{0:T(128)} %bitcast.upper_ref, s32[1]{0:T(128)} %bitcast.1.at_ref, bf16[1024,1536]{1,0:T(8,128)(2,1)} %bitcast.6, bf16[1024,1536]{1,0:T(8,128)(2,1)} %bitcast.7, bf16[1,2048,512]{2,1,0:T(8,128)(2,1)} %weight_ref.1, f32[1,2048]{1,0:T(1,128)} %gain_ref.1), custom_call_target="tpu_custom_call" | custom-call | flops 1073741824 | bytes 5242880 | tf_op jit(solution)/shard_map/product/pallas_call | solution.py:103
  93.2 6.0 %collective-permute-start = (bf16[1024,256]{1,0:T(8,128)(2,1)}, bf16[1024,256]{1,0:T(8,128)(2,1)S(1)}, u32[]{:S(2)}, u32[]{:S(2)}) collective-permute-start(bf16[1024,256]{1,0:T(8,128)(2,1)} %get-tuple-element.6), channel_id=1, source_target_pairs={{0,256},{8,264},{16,272},{24,280},{32,288},{40,296},{48,304},{56,3... | collective-permute-start | bytes 1572872 | tf_op jit(solution)/shard_map/ppermute | solution.py:159
  99.2 3.8 %collective-permute-start.1 = (f32[1,1024]{1,0:T(1,128)}, f32[1,1024]{1,0:T(1,128)S(1)}, u32[]{:S(2)}, u32[]{:S(2)}) collective-permute-start(f32[1,1024]{1,0:T(1,128)} %get-tuple-element.7), channel_id=1, source_target_pairs={{0,256},{8,264},{16,272},{24,280},{32,288},{40,296},{48,304},{56,3... | collective-permute-start | bytes 12296 | tf_op jit(solution)/shard_map/ppermute | solution.py:163
  103.0 21.3 %collective-permute-done.1 = f32[1,1024]{1,0:T(1,128)S(1)} collective-permute-done((f32[1,1024]{1,0:T(1,128)}, f32[1,1024]{1,0:T(1,128)S(1)}, u32[]{:S(2)}, u32[]{:S(2)}) %collective-permute-start.1) | collective-permute-done | bytes 4128 | tf_op jit(solution)/shard_map/ppermute | solution.py:163
  124.3 0.7 add.8
  124.9 1.9 %collective-permute-start.2 = (f32[1,1024]{1,0:T(1,128)S(1)}, f32[1,1024]{1,0:T(1,128)S(1)}, u32[]{:S(2)}, u32[]{:S(2)}) collective-permute-start(f32[1,1024]{1,0:T(1,128)S(1)} %add.8), channel_id=1, source_target_pairs={{0,1},{1,0},{2,3},{3,2},{4,5},{5,4},{6,7},{7,6},{8,9},{9,8},{10,11... | collective-permute-start | bytes 12296 | tf_op jit(solution)/shard_map/ppermute | solution.py:164
  126.9 7.5 %collective-permute-done.2 = f32[1,1024]{1,0:T(1,128)S(1)} collective-permute-done((f32[1,1024]{1,0:T(1,128)S(1)}, f32[1,1024]{1,0:T(1,128)S(1)}, u32[]{:S(2)}, u32[]{:S(2)}) %collective-permute-start.2) | collective-permute-done | bytes 4128 | tf_op jit(solution)/shard_map/ppermute | solution.py:164
  134.3 0.6 broadcast_select_fusion
  134.9 0.0 collective-permute-done
  135.0 2.1 %fusion = bf16[1,1024,256]{2,1,0:T(8,128)(2,1)} fusion(f32[1024,256]{1,0:T(8,128)} %get-tuple-element.5, bf16[1024,256]{1,0:T(8,128)(2,1)S(1)} %collective-permute-done), kind=kLoop, calls=%fused_computation.1 | loop fusion | flops 786432 | bytes 2097152 | tf_op jit(solution)/shard_map/broadcast_in_dim | solution.py:173
Async XLA Ops:
  5.7 80.4 %all-to-all-start = ((bf16[8,128,1536]{2,1,0:T(8,128)(2,1)}), bf16[8,128,1536]{2,1,0:T(8,128)(2,1)S(1)}, u32[]{:S(2)}, u32[]{:S(2)}) async-start(bf16[8,128,1536]{2,1,0:T(8,128)(2,1)} %split.1), calls=%async_computation | async-start | bytes 6291456 | tf_op jit(solution)/shard_map/all_to_all | solution.py:149
  86.1 1.7 %copy-start = (bf16[8,128,1536]{2,1,0:T(8,128)(2,1)}, bf16[8,128,1536]{2,1,0:T(8,128)(2,1)S(1)}, u32[]{:S(2)}) copy-start(bf16[8,128,1536]{2,1,0:T(8,128)(2,1)S(1)} %all-to-all-done) | copy-start | bytes 9437188
  93.2 41.7 %collective-permute-start = (bf16[1024,256]{1,0:T(8,128)(2,1)}, bf16[1024,256]{1,0:T(8,128)(2,1)S(1)}, u32[]{:S(2)}, u32[]{:S(2)}) collective-permute-start(bf16[1024,256]{1,0:T(8,128)(2,1)} %get-tuple-element.6), channel_id=1, source_target_pairs={{0,256},{8,264},{16,272},{24,280},{32,288},{40,296},{48,304},{56,3... | collective-permute-start | bytes 1572872 | tf_op jit(solution)/shard_map/ppermute | solution.py:159
  99.2 25.1 %collective-permute-start.1 = (f32[1,1024]{1,0:T(1,128)}, f32[1,1024]{1,0:T(1,128)S(1)}, u32[]{:S(2)}, u32[]{:S(2)}) collective-permute-start(f32[1,1024]{1,0:T(1,128)} %get-tuple-element.7), channel_id=1, source_target_pairs={{0,256},{8,264},{16,272},{24,280},{32,288},{40,296},{48,304},{56,3... | collective-permute-start | bytes 12296 | tf_op jit(solution)/shard_map/ppermute | solution.py:163
  124.9 9.4 %collective-permute-start.2 = (f32[1,1024]{1,0:T(1,128)S(1)}, f32[1,1024]{1,0:T(1,128)S(1)}, u32[]{:S(2)}, u32[]{:S(2)}) collective-permute-start(f32[1,1024]{1,0:T(1,128)S(1)} %add.8), channel_id=1, source_target_pairs={{0,1},{1,0},{2,3},{3,2},{4,5},{5,4},{6,7},{7,6},{8,9},{9,8},{10,11... | collective-permute-start | bytes 12296 | tf_op jit(solution)/shard_map/ppermute | solution.py:164

commit v2 on v0

v2 whole, which is shorter than its diff:
```python
import functools

import jax
import jax.numpy as jnp
from jax import lax
from jax.experimental import pallas as pl
from jax.experimental.pallas import tpu as pltpu
from jax.sharding import PartitionSpec as P

GROUP = ("fsdp", "dp")
TILE = 128
EPS = 1e-05
ADDCOST = 1 << 20
VLIM = 20
HBM = pl.BlockSpec(memory_space=pltpu.HBM)
VMEM = pl.BlockSpec(memory_space=pltpu.VMEM)
SMEM = pl.BlockSpec(memory_space=pltpu.SMEM)


def params():
    return pltpu.CompilerParams(vmem_limit_bytes=VLIM << 20)


def cost(size=0):
    return pl.CostEstimate(flops=0, bytes_accessed=size, transcendentals=0)


def split_kernel(
    order_ref, upper_ref, acts_ref, cot_ref, first_ref, second_ref,
    acts_own, cot_own, send_own, keep_own, acts_sem, cot_sem, move_sem, send_sem, keep_sem,
):
    groups = first_ref.shape[0]
    _, batches, tokens, width = acts_ref.shape
    slab = width // groups
    half = cot_ref.shape[-1] // 2
    load_cot = pltpu.make_async_copy(cot_ref.at[0], cot_own, cot_sem)
    load_cot.start()
    loads, moves = [], []
    for m in range(batches):
        loads.append(pltpu.make_async_copy(acts_ref.at[0, m], acts_own.at[m], acts_sem.at[m]))
        loads[-1].start()
    load_cot.wait()
    keep_at = pl.multiple_of(upper_ref[0] * half, 128)
    send_at = pl.multiple_of((1 - upper_ref[0]) * half, 128)
    for m in range(batches):
        loads[m].wait()
        for q in range(groups):
            moves.append(
                pltpu.make_async_copy(
                    acts_own.at[m, :, pl.ds(q * slab, slab)],
                    first_ref.at[q, pl.ds(m * tokens, tokens), pl.ds(half, slab)],
                    move_sem.at[m, q],
                )
            )
            moves[-1].start()
        squares = jnp.zeros((tokens, 128), jnp.float32)
        for c in range(0, width, 128):
            part = acts_own[m, :, c : c + 128].astype(jnp.float32)
            squares += part * part
        rstd = lax.rsqrt(jnp.sum(squares, axis=-1, keepdims=True) / width + EPS)
        slot = jnp.int32(0)
        for j in range(1, batches):
            slot = jnp.where(order_ref[j] == m, jnp.int32(j), slot)
        rows = pl.ds(m * tokens, tokens)
        send_own[rows, :] = (cot_own[slot, :, pl.ds(send_at, half)].astype(jnp.float32) * rstd).astype(jnp.bfloat16)
        keep_own[rows, :] = (cot_own[slot, :, pl.ds(keep_at, half)].astype(jnp.float32) * rstd).astype(jnp.bfloat16)
    for q in range(groups):
        moves.append(pltpu.make_async_copy(send_own, first_ref.at[q, :, pl.ds(0, half)], send_sem.at[q]))
        moves[-1].start()
        moves.append(pltpu.make_async_copy(keep_own, second_ref.at[q], keep_sem.at[q]))
        moves[-1].start()
    for move in moves:
        move.wait()


def split(acts, cotangent, order, upper, groups):
    _, batches, tokens, width = acts.shape
    keys = cotangent.shape[-1]
    half = keys // 2
    sizes = (half + width // groups, half)
    dma = pltpu.SemaphoreType.DMA
    return pl.pallas_call(
        split_kernel,
        out_shape=tuple(jax.ShapeDtypeStruct((groups, batches * tokens, n), jnp.bfloat16) for n in sizes),
        in_specs=[SMEM, SMEM, HBM, HBM],
        out_specs=(HBM, HBM),
        scratch_shapes=[
            pltpu.VMEM((batches, tokens, width), jnp.bfloat16),
            pltpu.VMEM((batches, tokens, keys), jnp.bfloat16),
            pltpu.VMEM((batches * tokens, half), jnp.bfloat16),
            pltpu.VMEM((batches * tokens, half), jnp.bfloat16),
            dma((batches,)),
            dma,
            dma((batches, groups)),
            dma((groups,)),
            dma((groups,)),
        ],
        cost_estimate=cost(5 << 20),
        name="split",
    )(order.reshape(-1), upper, acts, cotangent)


def half_product(block_ref, grads, at, half):
    return lax.dot_general(
        block_ref[:, half + at : half + at + TILE], grads, (((0,), (0,)), ((), ())), preferred_element_type=jnp.float32
    )


def gain_terms(total, weight):
    terms = total * weight.astype(jnp.float32)
    folded = terms[:, :128]
    for c in range(128, terms.shape[1], 128):
        folded += terms[:, c : c + 128]
    return jnp.sum(folded.T, axis=0, keepdims=True)


def fetch_weight(weight_ref, own_ref, sem, first, column):
    rows, half = own_ref.shape
    copy = pltpu.make_async_copy(weight_ref.at[0, pl.ds(first, rows), pl.ds(column, half)], own_ref, sem)
    copy.start()
    return copy


def send_kernel(upper_ref, replica_ref, block_ref, weight_ref, gain_ref, send_ref, gterm_ref, own_ref, total_ref, sem):
    rows, half = own_ref.shape
    first = pl.multiple_of(replica_ref[0] * rows, rows)
    fetch = fetch_weight(weight_ref, own_ref, sem, first, pl.multiple_of((1 - upper_ref[0]) * half, half))
    grads = block_ref[:, :half]
    for at in range(0, rows, TILE):
        total = half_product(block_ref, grads, at, half)
        gain = gain_ref[:, pl.ds(pl.multiple_of(first + at, 128), TILE)].reshape(TILE, 1)
        send_ref[at : at + TILE, :] = (total * gain).astype(jnp.bfloat16)
        total_ref[at : at + TILE, :] = total
    fetch.wait()
    for at in range(0, rows, TILE):
        gterm_ref[:, at : at + TILE] = gain_terms(total_ref[at : at + TILE, :], own_ref[at : at + TILE, :])


def gain_kernel(upper_ref, replica_ref, before_ref, grads_ref, block_ref, weight_ref, gterm_ref, own_ref, total_ref, sem):
    rows, half = own_ref.shape
    first = pl.multiple_of(replica_ref[0] * rows, rows)
    fetch = fetch_weight(weight_ref, own_ref, sem, first, pl.multiple_of(upper_ref[0] * half, half))
    gterm_ref[...] = jnp.zeros_like(gterm_ref)
    grads = grads_ref[...]
    for at in range(0, rows, TILE):
        total_ref[at : at + TILE, :] = half_product(block_ref, grads, at, half)
    fetch.wait()
    for at in range(0, rows, TILE):
        gterm = gain_terms(total_ref[at : at + TILE, :], own_ref[at : at + TILE, :])
        gterm_ref[:, pl.ds(pl.multiple_of(first + at, 128), TILE)] = gterm + before_ref[:, at : at + TILE]


def finish_kernel(replica_ref, grads_ref, block_ref, gain_ref, arrived_ref, out_ref):
    rows, half = arrived_ref.shape
    first = pl.multiple_of(replica_ref[0] * rows, rows)
    grads = grads_ref[...]
    for at in range(0, rows, TILE):
        gain = gain_ref[:, pl.ds(pl.multiple_of(first + at, 128), TILE)].reshape(TILE, 1)
        keep = half_product(block_ref, grads, at, half) * gain
        out_ref[0, at : at + TILE, :] = (keep + arrived_ref[at : at + TILE, :].astype(jnp.float32)).astype(jnp.bfloat16)


def local(acts, cotangent, order, key_weight, gain):
    groups = lax.axis_size(GROUP)
    slab = acts.shape[-1] // groups
    tokens = acts.shape[1] * acts.shape[2]
    half = cotangent.shape[-1] // 2
    ranks = lax.axis_size("pipe")
    middle = ranks // 2
    upper = (lax.axis_index("pipe") >= middle).astype(jnp.int32).reshape(1)
    replica = lax.axis_index("dp").reshape(1)
    across = [(i, (i + middle) % ranks) for i in range(ranks)]
    pairs = [[i, i + middle] for i in range(middle)]

    def exchange(block):
        return lax.all_to_all(block, GROUP, 0, 0, tiled=True).reshape(groups * tokens, -1)

    key_weight = pltpu.with_memory_space_constraint(key_weight, pltpu.HBM)
    first, second = split(acts, cotangent, order, upper, groups)
    block = exchange(first)
    second, block = lax.optimization_barrier((second, block))
    grads = exchange(second)
    scratch = [
        pltpu.VMEM((slab, half), jnp.bfloat16),
        pltpu.VMEM((slab, half), jnp.float32),
        pltpu.SemaphoreType.DMA,
    ]
    send, gterm = pl.pallas_call(
        send_kernel,
        out_shape=(jax.ShapeDtypeStruct((slab, half), jnp.bfloat16), jax.ShapeDtypeStruct((1, slab), jnp.float32)),
        in_specs=[SMEM, SMEM, VMEM, HBM, VMEM],
        out_specs=(VMEM, VMEM),
        scratch_shapes=scratch,
        cost_estimate=cost(),
        compiler_params=params(),
        name="send",
    )(upper, replica, block, key_weight, gain)
    arrived = lax.ppermute(send, "pipe", across)
    gown = pl.pallas_call(
        gain_kernel,
        out_shape=jax.ShapeDtypeStruct(gain.shape, jnp.float32),
        in_specs=[SMEM, SMEM, VMEM, VMEM, VMEM, HBM],
        out_specs=VMEM,
        scratch_shapes=scratch,
        cost_estimate=cost(),
        compiler_params=params(),
        name="gain",
    )(upper, replica, gterm, grads, block, key_weight)
    gain_pair = lax.psum(lax.psum(gown, "dp"), "pipe", axis_index_groups=pairs)
    weight_out = pl.pallas_call(
        finish_kernel,
        out_shape=jax.ShapeDtypeStruct((1, slab, half), jnp.bfloat16),
        in_specs=[SMEM, VMEM, VMEM, VMEM, VMEM],
        out_specs=VMEM,
        cost_estimate=cost(ADDCOST),
        compiler_params=params(),
        name="finish",
    )(replica, grads, block, gain, arrived)
    return (weight_out, gain_pair)


def solution(mesh):
    return jax.shard_map(
        local,
        mesh=mesh,
        in_specs=(
            P("pipe", None, GROUP, None),
            P("pipe", None, GROUP, None),
            P("pipe", GROUP, None),
            P("pipe", "fsdp", None),
            P("pipe", "fsdp"),
        ),
        out_specs=(P("pipe", GROUP, None), P("pipe", "fsdp")),
        check_vma=False,
    )
```

time: 341 us -> 120 us (0.35)
  the two profiles are of different devices: /device:TPU:2 before, /device:TPU:68 now
where the time goes in v2:
time: 120 us
  blocking collectives  91.4 us (76%)
  starting transfers between devices  11.4 us (10%)
  Pallas kernels  11.3 us (9%)
  waiting for transfers between devices  4.88 us (4%)
    all_to_all x1, blocking collectives, exchange(): lax.all_to_all(block, GROUP, 0, 0, tiled=True).reshape(groups * tokens, -1)  70.6 us
    psum x2, blocking collectives, local(): gain_pair = lax.psum(lax.psum(gown, 'dp'), 'pipe', axis_index_groups=pairs)  20.8 us
    ppermute x1, starting transfers between devices, local(): arrived = lax.ppermute(send, 'pipe', across)  7.73 us
    all_to_all x1, waiting for transfers between devices, exchange(): lax.all_to_all(block, GROUP, 0, 0, tiled=True).reshape(groups * tokens, -1)  4.88 us
    pallas_call x1, Pallas kernels, split(): pl.pallas_call(split_kernel, out_shape=tuple((jax.ShapeDtypeStruct((group...  4.34 us
    all_to_all x1, starting transfers between devices, exchange(): lax.all_to_all(block, GROUP, 0, 0, tiled=True).reshape(groups * tokens, -1)  3.65 us
    pallas_call x1, Pallas kernels, local(): pl.pallas_call(finish_kernel, out_shape=jax.ShapeDtypeStruct((1, slab, ha...  2.63 us
    pallas_call x1, Pallas kernels, local(): pl.pallas_call(send_kernel, out_shape=(jax.ShapeDtypeStruct((slab, half),...  2.52 us
  transfers between devices with their start and end apart: 2, of which 1 were waited for; matrix products, arithmetic and copies ran while one was open for 0% of the time, Pallas kernels for 2%

profile of v2, /device:TPU:68, one launch (start us, length us, event | category | flops | bytes accessed | tf_op | source)
XLA Modules:
  0.0 119.7 jit_solution(14048071164089732)
XLA Ops:
  0.6 4.3 %split.1 = (bf16[8,128,1280]{2,1,0:T(8,128)(2,1)}, bf16[8,128,256]{2,1,0:T(8,128)(2,1)}) custom-call(s32[4]{0:T(128)} %bitcast.10, s32[1]{0:T(128)} %bitcast.2.upper_ref, bf16[1,4,32,8192]{3,2,1,0:T(8,128)(2,1)} %acts_ref.1, bf16[1,4,32,512]{3,2,1,0:T(8,128)(2,1)} %cot_ref.1), custom_call_target="tpu_custom_call" | custom-call | bytes 5242880 | tf_op jit(solution)/shard_map/split/pallas_call | solution.py:82
  5.0 0.0 copy-start
  5.0 70.6 %all_to_all.10 = bf16[8,128,1280]{2,1,0:T(8,128)(2,1)S(1)} all-to-all(bf16[8,128,1280]{2,1,0:T(8,128)(2,1)} %get-tuple-element.9), channel_id=1, replica_groups=mesh['pipe'=64,'fsdp'=4,'dp'=2] {'fsdp','dp'}, dimensions={0} | all-to-all | bytes 5242880 | tf_op jit(solution)/shard_map/all_to_all | solution.py:176
  75.6 3.7 %all-to-all-start.1 = ((bf16[8,128,256]{2,1,0:T(8,128)(2,1)}), bf16[8,128,256]{2,1,0:T(8,128)(2,1)S(1)}, u32[]{:S(2)}, u32[]{:S(2)}) async-start(bf16[8,128,256]{2,1,0:T(8,128)(2,1)} %get-tuple-element.10), calls=%async_computation.1 | async-start | bytes 1048576 | tf_op jit(solution)/shard_map/all_to_all | solution.py:176
  79.2 0.0 copy-done
  79.2 2.5 %send.1 = (bf16[1024,256]{1,0:T(8,128)(2,1)}, f32[1,1024]{1,0:T(1,128)S(1)}) custom-call(s32[1]{0:T(128)} %bitcast.2.upper_ref, s32[1]{0:T(128)} %bitcast.replica_ref, bf16[1024,1280]{1,0:T(8,128)(2,1)S(1)} %bitcast.5, bf16[1,2048,512]{2,1,0:T(8,128)(2,1)} %weight_ref.3, f32[1,2048]{1,0:T(1,128)S(1)} %copy-done), custom_call_target="tpu_custom_call" | custom-call | tf_op jit(solution)/shard_map/send/pallas_call | solution.py:188
  81.8 7.7 %collective-permute-start = (bf16[1024,256]{1,0:T(8,128)(2,1)}, bf16[1024,256]{1,0:T(8,128)(2,1)}, u32[]{:S(2)}, u32[]{:S(2)}) collective-permute-start(bf16[1024,256]{1,0:T(8,128)(2,1)} %get-tuple-element.12), channel_id=1, source_target_pairs={{0,256},{8,264},{16,272},{24,280},{32,288},{40,296},{48,304},{56,3... | collective-permute-start | bytes 1572872 | tf_op jit(solution)/shard_map/ppermute | solution.py:198
  89.5 4.9 %all-to-all-done.1 = bf16[8,128,256]{2,1,0:T(8,128)(2,1)S(1)} async-done(((bf16[8,128,256]{2,1,0:T(8,128)(2,1)}), bf16[8,128,256]{2,1,0:T(8,128)(2,1)S(1)}, u32[]{:S(2)}, u32[]{:S(2)}) %all-to-all-start.1) | async-done | bytes 524320 | tf_op jit(solution)/shard_map/all_to_all | solution.py:176
  94.4 1.8 %gain.1 = f32[1,2048]{1,0:T(1,128)S(1)} custom-call(s32[1]{0:T(128)} %bitcast.2.upper_ref, s32[1]{0:T(128)} %bitcast.replica_ref, f32[1,1024]{1,0:T(1,128)S(1)} %get-tuple-element.13.before_ref, bf16[1024,256]{1,0:T(8,128)(2,1)S(1)} %bitcast.8, bf16[1024,1280]{1,0:T(8,128)(2,1)S(1)} %bitcast.6, bf16[1,2048,512]{2,1,0:T(8,128)(2,1)} %weight_ref.3), custom_call_target="tpu_custom_call" | custom-call | tf_op jit(solution)/shard_map/gain/pallas_call | solution.py:199
  96.3 8.9 %psum.14 = f32[1,2048]{1,0:T(1,128)S(1)} all-reduce(f32[1,2048]{1,0:T(1,128)S(1)} %gain.1), channel_id=1, replica_groups=mesh['pipe'=64,'fsdp'=4,'dp'=2] {'dp'}, use_global_device_ids=true, to_apply=%region_0.0 | all-reduce | flops 2048 | bytes 16384 | tf_op jit(solution)/shard_map/psum | solution.py:209
  105.2 11.9 %psum.15 = f32[1,2048]{1,0:T(1,128)} all-reduce(f32[1,2048]{1,0:T(1,128)S(1)} %psum.14), channel_id=1, replica_groups={{0,256},{8,264},{16,272},{24,280},{32,288},{40,296},{48,304},{56,312},{..., use_global_device_ids=true, to_apply=%region_1.0 | all-reduce | flops 2048 | bytes 16384 | tf_op jit(solution)/shard_map/psum | solution.py:209
  117.1 0.0 collective-permute-done.arrived_ref
  117.1 2.6 %finish.1 = bf16[1,1024,256]{2,1,0:T(8,128)(2,1)} custom-call(s32[1]{0:T(128)} %bitcast.replica_ref, bf16[1024,256]{1,0:T(8,128)(2,1)S(1)} %bitcast.9, bf16[1024,1280]{1,0:T(8,128)(2,1)S(1)} %bitcast.7, f32[1,2048]{1,0:T(1,128)S(1)} %copy-done, bf16[1024,256]{1,0:T(8,128)(2,1)} %collective-permute-done.arrived_ref), custom_call_target="tpu_custom_call" | custom-call | bytes 1048576 | tf_op jit(solution)/shard_map/finish/pallas_call | solution.py:210
Async XLA Ops:
  5.0 74.3 %copy-start = (f32[1,2048]{1,0:T(1,128)S(1)}, f32[1,2048]{1,0:T(1,128)}, u32[]{:S(2)}) copy-start(f32[1,2048]{1,0:T(1,128)} %gain_ref.3) | copy-start | bytes 24580
  75.6 18.8 %all-to-all-start.1 = ((bf16[8,128,256]{2,1,0:T(8,128)(2,1)}), bf16[8,128,256]{2,1,0:T(8,128)(2,1)S(1)}, u32[]{:S(2)}, u32[]{:S(2)}) async-start(bf16[8,128,256]{2,1,0:T(8,128)(2,1)} %get-tuple-element.10), calls=%async_computation.1 | async-start | bytes 1048576 | tf_op jit(solution)/shard_map/all_to_all | solution.py:176
  81.8 35.3 %collective-permute-start = (bf16[1024,256]{1,0:T(8,128)(2,1)}, bf16[1024,256]{1,0:T(8,128)(2,1)}, u32[]{:S(2)}, u32[]{:S(2)}) collective-permute-start(bf16[1024,256]{1,0:T(8,128)(2,1)} %get-tuple-element.12), channel_id=1, source_target_pairs={{0,256},{8,264},{16,272},{24,280},{32,288},{40,296},{48,304},{56,3... | collective-permute-start | bytes 1572872 | tf_op jit(solution)/shard_map/ppermute | solution.py:198

commit v3 on v2

--- a/solution.py
+++ b/solution.py
@@ -8,13 +8,16 @@
 from jax.sharding import PartitionSpec as P
 
 GROUP = ("fsdp", "dp")
-TILE = 128
+TILE = 256
+SPLIT = 80
+STEPS = 4
 EPS = 1e-05
 ADDCOST = 1 << 20
 VLIM = 20
 HBM = pl.BlockSpec(memory_space=pltpu.HBM)
 VMEM = pl.BlockSpec(memory_space=pltpu.VMEM)
 SMEM = pl.BlockSpec(memory_space=pltpu.SMEM)
+ARRIVED = pl.BlockSpec(memory_space=pl.ANY)
 
 
 def params():
@@ -27,50 +30,44 @@
 
 def split_kernel(
     order_ref, upper_ref, acts_ref, cot_ref, first_ref, second_ref,
-    acts_own, cot_own, send_own, keep_own, acts_sem, cot_sem, move_sem, send_sem, keep_sem,
+    acts_own, cot_own, keep_own, acts_sem, cot_sem, keep_sem,
 ):
     groups = first_ref.shape[0]
     _, batches, tokens, width = acts_ref.shape
     slab = width // groups
     half = cot_ref.shape[-1] // 2
+    copies = [pltpu.make_async_copy(acts_ref.at[0, m], acts_own.at[m], acts_sem.at[m]) for m in range(batches)]
     load_cot = pltpu.make_async_copy(cot_ref.at[0], cot_own, cot_sem)
+    for load in copies:
+        load.start()
     load_cot.start()
-    loads, moves = [], []
-    for m in range(batches):
-        loads.append(pltpu.make_async_copy(acts_ref.at[0, m], acts_own.at[m], acts_sem.at[m]))
-        loads[-1].start()
-    load_cot.wait()
     keep_at = pl.multiple_of(upper_ref[0] * half, 128)
     send_at = pl.multiple_of((1 - upper_ref[0]) * half, 128)
+    stores = []
     for m in range(batches):
-        loads[m].wait()
-        for q in range(groups):
-            moves.append(
-                pltpu.make_async_copy(
-                    acts_own.at[m, :, pl.ds(q * slab, slab)],
-                    first_ref.at[q, pl.ds(m * tokens, tokens), pl.ds(half, slab)],
-                    move_sem.at[m, q],
-                )
-            )
-            moves[-1].start()
+        copies[m].wait()
+        rows = slice(m * tokens, (m + 1) * tokens)
         squares = jnp.zeros((tokens, 128), jnp.float32)
         for c in range(0, width, 128):
-            part = acts_own[m, :, c : c + 128].astype(jnp.float32)
-            squares += part * part
+            floats = acts_own[m, :, c : c + 128].astype(jnp.float32)
+            squares += floats * floats
         rstd = lax.rsqrt(jnp.sum(squares, axis=-1, keepdims=True) / width + EPS)
+        if m == 0:
+            load_cot.wait()
         slot = jnp.int32(0)
         for j in range(1, batches):
-            slot = jnp.where(order_ref[j] == m, jnp.int32(j), slot)
-        rows = pl.ds(m * tokens, tokens)
-        send_own[rows, :] = (cot_own[slot, :, pl.ds(send_at, half)].astype(jnp.float32) * rstd).astype(jnp.bfloat16)
-        keep_own[rows, :] = (cot_own[slot, :, pl.ds(keep_at, half)].astype(jnp.float32) * rstd).astype(jnp.bfloat16)
-    for q in range(groups):
-        moves.append(pltpu.make_async_copy(send_own, first_ref.at[q, :, pl.ds(0, half)], send_sem.at[q]))
-        moves[-1].start()
-        moves.append(pltpu.make_async_copy(keep_own, second_ref.at[q], keep_sem.at[q]))
-        moves[-1].start()
-    for move in moves:
-        move.wait()
+            slot = jnp.where(order_ref[0, 0, j] == m, jnp.int32(j), slot)
+        send = (cot_own[slot, :, pl.ds(send_at, half)].astype(jnp.float32) * rstd).astype(jnp.bfloat16)
+        keep = (cot_own[slot, :, pl.ds(keep_at, half)].astype(jnp.float32) * rstd).astype(jnp.bfloat16)
+        for q in range(groups):
+            keep_own[q, rows, :] = keep
+        stores.append(pltpu.make_async_copy(keep_own.at[:, rows], second_ref.at[:, rows], keep_sem.at[m]))
+        stores[-1].start()
+        for q in range(groups):
+            first_ref[q, rows, :half] = send
+            first_ref[q, rows, half:] = acts_own[m, :, q * slab : (q + 1) * slab]
+    for store in stores:
+        store.wait()
 
 
 def split(acts, cotangent, order, upper, groups):
@@ -78,26 +75,24 @@
     keys = cotangent.shape[-1]
     half = keys // 2
     sizes = (half + width // groups, half)
-    dma = pltpu.SemaphoreType.DMA
+    acts, cotangent, order = (pltpu.with_memory_space_constraint(x, pltpu.HBM) for x in (acts, cotangent, order))
     return pl.pallas_call(
         split_kernel,
         out_shape=tuple(jax.ShapeDtypeStruct((groups, batches * tokens, n), jnp.bfloat16) for n in sizes),
         in_specs=[SMEM, SMEM, HBM, HBM],
-        out_specs=(HBM, HBM),
+        out_specs=(VMEM, HBM),
         scratch_shapes=[
             pltpu.VMEM((batches, tokens, width), jnp.bfloat16),
             pltpu.VMEM((batches, tokens, keys), jnp.bfloat16),
-            pltpu.VMEM((batches * tokens, half), jnp.bfloat16),
-            pltpu.VMEM((batches * tokens, half), jnp.bfloat16),
-            dma((batches,)),
-            dma,
-            dma((batches, groups)),
-            dma((groups,)),
-            dma((groups,)),
+            pltpu.VMEM((groups, batches * tokens, half), jnp.bfloat16),
+            pltpu.SemaphoreType.DMA((batches,)),
+            pltpu.SemaphoreType.DMA,
+            pltpu.SemaphoreType.DMA((batches,)),
         ],
         cost_estimate=cost(5 << 20),
+        compiler_params=pltpu.CompilerParams(vmem_limit_bytes=SPLIT << 18),
         name="split",
-    )(order.reshape(-1), upper, acts, cotangent)
+    )(order, upper, acts, cotangent)
 
 
 def half_product(block_ref, grads, at, half):
@@ -150,14 +145,33 @@
         gterm_ref[:, pl.ds(pl.multiple_of(first + at, 128), TILE)] = gterm + before_ref[:, at : at + TILE]
 
 
-def finish_kernel(replica_ref, grads_ref, block_ref, gain_ref, arrived_ref, out_ref):
-    rows, half = arrived_ref.shape
+def keep_kernel(replica_ref, after_ref, grads_ref, block_ref, gain_ref, keep_ref):
+    del after_ref
+    rows, half = keep_ref.shape
     first = pl.multiple_of(replica_ref[0] * rows, rows)
     grads = grads_ref[...]
     for at in range(0, rows, TILE):
         gain = gain_ref[:, pl.ds(pl.multiple_of(first + at, 128), TILE)].reshape(TILE, 1)
-        keep = half_product(block_ref, grads, at, half) * gain
-        out_ref[0, at : at + TILE, :] = (keep + arrived_ref[at : at + TILE, :].astype(jnp.float32)).astype(jnp.bfloat16)
+        keep_ref[at : at + TILE, :] = half_product(block_ref, grads, at, half) * gain
+
+
+def add_kernel(keep_ref, arrived_ref, out_ref, arrived_own, out_own, load_sem, store_sem):
+    rows = keep_ref.shape[0] // STEPS
+    bands = [pl.ds(n * rows, rows) for n in range(STEPS)]
+    loads = [
+        pltpu.make_async_copy(arrived_ref.at[band], arrived_own.at[band], load_sem.at[n]) for n, band in enumerate(bands)
+    ]
+    stores = [
+        pltpu.make_async_copy(out_own.at[band], out_ref.at[0, band], store_sem.at[n]) for n, band in enumerate(bands)
+    ]
+    for load in loads:
+        load.start()
+    for band, load, store in zip(bands, loads, stores):
+        load.wait()
+        out_own[band, :] = (keep_ref[band, :] + arrived_own[band, :].astype(jnp.float32)).astype(jnp.bfloat16)
+        store.start()
+    for store in stores:
+        store.wait()
 
 
 def local(acts, cotangent, order, key_weight, gain):
@@ -170,7 +184,6 @@
     upper = (lax.axis_index("pipe") >= middle).astype(jnp.int32).reshape(1)
     replica = lax.axis_index("dp").reshape(1)
     across = [(i, (i + middle) % ranks) for i in range(ranks)]
-    pairs = [[i, i + middle] for i in range(middle)]
 
     def exchange(block):
         return lax.all_to_all(block, GROUP, 0, 0, tiled=True).reshape(groups * tokens, -1)
@@ -206,17 +219,33 @@
         compiler_params=params(),
         name="gain",
     )(upper, replica, gterm, grads, block, key_weight)
-    gain_pair = lax.psum(lax.psum(gown, "dp"), "pipe", axis_index_groups=pairs)
+    gboth = gown + lax.ppermute(gown, "dp", [(0, 1), (1, 0)])
+    there = lax.ppermute(gboth, "pipe", across)
+    keep = pl.pallas_call(
+        keep_kernel,
+        out_shape=jax.ShapeDtypeStruct((slab, half), jnp.float32),
+        in_specs=[SMEM, pl.BlockSpec(memory_space=pl.ANY), VMEM, VMEM, VMEM],
+        out_specs=VMEM,
+        cost_estimate=cost(),
+        compiler_params=params(),
+        name="keep",
+    )(replica, gboth, grads, block, gain)
     weight_out = pl.pallas_call(
-        finish_kernel,
+        add_kernel,
         out_shape=jax.ShapeDtypeStruct((1, slab, half), jnp.bfloat16),
-        in_specs=[SMEM, VMEM, VMEM, VMEM, VMEM],
-        out_specs=VMEM,
+        in_specs=[VMEM, ARRIVED],
+        out_specs=HBM,
+        scratch_shapes=[
+            pltpu.VMEM((slab, half), jnp.bfloat16),
+            pltpu.VMEM((slab, half), jnp.bfloat16),
+            pltpu.SemaphoreType.DMA((STEPS,)),
+            pltpu.SemaphoreType.DMA((STEPS,)),
+        ],
         cost_estimate=cost(ADDCOST),
         compiler_params=params(),
-        name="finish",
-    )(replica, grads, block, gain, arrived)
-    return (weight_out, gain_pair)
+        name="add",
+    )(keep, arrived)
+    return (weight_out, gboth + there)
 
 
 def solution(mesh):

time: 120 us -> 116 us (0.967)
  the two profiles are of different devices: /device:TPU:68 before, /device:TPU:70 now
where the time goes in v3:
time: 116 us; the launch traced here: 115 us
  blocking collectives  70.5 us (61%)
  starting transfers between devices  23.9 us (21%)
  waiting for transfers between devices  10.4 us (9%)
  Pallas kernels  9.16 us (8%)
    all_to_all x1, blocking collectives, exchange(): lax.all_to_all(block, GROUP, 0, 0, tiled=True).reshape(groups * tokens, -1)  70.5 us
    ppermute x1, starting transfers between devices, local(): arrived = lax.ppermute(send, 'pipe', across)  7.74 us
    ppermute x1, starting transfers between devices, local(): there = lax.ppermute(gboth, 'pipe', across)  7.73 us
    all_to_all x1, waiting for transfers between devices, exchange(): lax.all_to_all(block, GROUP, 0, 0, tiled=True).reshape(groups * tokens, -1)  5.36 us
    ppermute x1, starting transfers between devices, local(): gboth = gown + lax.ppermute(gown, 'dp', [(0, 1), (1, 0)])  4.79 us
    ppermute x1, waiting for transfers between devices, local(): gboth = gown + lax.ppermute(gown, 'dp', [(0, 1), (1, 0)])  4.66 us
    all_to_all x1, starting transfers between devices, exchange(): lax.all_to_all(block, GROUP, 0, 0, tiled=True).reshape(groups * tokens, -1)  3.65 us
    pallas_call x1, Pallas kernels, split(): pl.pallas_call(split_kernel, out_shape=tuple((jax.ShapeDtypeStruct((group...  3.23 us
  transfers between devices with their start and end apart: 4, of which 3 were waited for; matrix products, arithmetic and copies ran while one was open for 0% of the time, Pallas kernels for 3%

profile of v3, /device:TPU:70, one launch (start us, length us, event | category | flops | bytes accessed | tf_op | source)
XLA Modules:
  0.0 115.3 jit_solution(15990082385880694961)
XLA Ops:
  0.6 3.2 %split.1 = (bf16[8,128,1280]{2,1,0:T(8,128)(2,1)S(1)}, bf16[8,128,256]{2,1,0:T(8,128)(2,1)S(1)}) custom-call(s32[1,1,4]{2,1,0:T(1,128)} %order_ref.1, s32[1]{0:T(128)} %bitcast.1.upper_ref, bf16[1,4,32,8192]{3,2,1,0:T(8,128)(2,1)} %acts_ref.1, bf16[1,4,32,512]{3,2,1,0:T(8,128)(2,1)} %cot_ref.1), custom_call_target="tpu_custom_call" | custom-call | bytes 5242880 | tf_op jit(solution)/shard_map/split/pallas_call | solution.py:79
  3.9 0.0 copy-start
  3.9 0.0 copy-start.1
  3.9 70.5 %all_to_all.10 = bf16[8,128,1280]{2,1,0:T(8,128)(2,1)S(1)} all-to-all(bf16[8,128,1280]{2,1,0:T(8,128)(2,1)S(1)} %get-tuple-element.9), channel_id=1, replica_groups=mesh['pipe'=64,'fsdp'=4,'dp'=2] {'fsdp','dp'}, dimensions={0} | all-to-all | bytes 5242880 | tf_op jit(solution)/shard_map/all_to_all | solution.py:189
  74.4 0.0 copy-done
  74.4 3.7 %all-to-all-start.1 = ((bf16[8,128,256]{2,1,0:T(8,128)(2,1)}), bf16[8,128,256]{2,1,0:T(8,128)(2,1)S(1)}, u32[]{:S(2)}, u32[]{:S(2)}) async-start(bf16[8,128,256]{2,1,0:T(8,128)(2,1)} %copy-done), calls=%async_computation.1 | async-start | bytes 1048576 | tf_op jit(solution)/shard_map/all_to_all | solution.py:189
  78.1 0.0 copy-done.1
  78.1 2.0 %send.1 = (bf16[1024,256]{1,0:T(8,128)(2,1)}, f32[1,1024]{1,0:T(1,128)S(1)}) custom-call(s32[1]{0:T(128)} %bitcast.1.upper_ref, s32[1]{0:T(128)} %bitcast.replica_ref, bf16[1024,1280]{1,0:T(8,128)(2,1)S(1)} %bitcast.4, bf16[1,2048,512]{2,1,0:T(8,128)(2,1)} %weight_ref.3, f32[1,2048]{1,0:T(1,128)S(1)} %copy-done.1), custom_call_target="tpu_custom_call" | custom-call | tf_op jit(solution)/shard_map/send/pallas_call | solution.py:201
  80.1 7.7 %collective-permute-start.1 = (bf16[1024,256]{1,0:T(8,128)(2,1)}, bf16[1024,256]{1,0:T(8,128)(2,1)}, u32[]{:S(2)}, u32[]{:S(2)}) collective-permute-start(bf16[1024,256]{1,0:T(8,128)(2,1)} %get-tuple-element.13), channel_id=1, source_target_pairs={{0,256},{8,264},{16,272},{24,280},{32,288},{40,296},{48,304},{56,3... | collective-permute-start | bytes 1572872 | tf_op jit(solution)/shard_map/ppermute | solution.py:211
  87.9 5.4 %all-to-all-done.1 = bf16[8,128,256]{2,1,0:T(8,128)(2,1)S(1)} async-done(((bf16[8,128,256]{2,1,0:T(8,128)(2,1)}), bf16[8,128,256]{2,1,0:T(8,128)(2,1)S(1)}, u32[]{:S(2)}, u32[]{:S(2)}) %all-to-all-start.1) | async-done | bytes 524320 | tf_op jit(solution)/shard_map/all_to_all | solution.py:189
  93.2 1.3 %gain.1 = f32[1,2048]{1,0:T(1,128)S(1)} custom-call(s32[1]{0:T(128)} %bitcast.1.upper_ref, s32[1]{0:T(128)} %bitcast.replica_ref, f32[1,1024]{1,0:T(1,128)S(1)} %get-tuple-element.11.before_ref, bf16[1024,256]{1,0:T(8,128)(2,1)S(1)} %bitcast.7, bf16[1024,1280]{1,0:T(8,128)(2,1)S(1)} %bitcast.5, bf16[1,2048,512]{2,1,0:T(8,128)(2,1)} %weight_ref.3), custom_call_target="tpu_custom_call" | custom-call | tf_op jit(solution)/shard_map/gain/pallas_call | solution.py:212
  94.5 4.8 %collective-permute-start = (f32[1,2048]{1,0:T(1,128)S(1)}, f32[1,2048]{1,0:T(1,128)S(1)}, u32[]{:S(2)}, u32[]{:S(2)}) collective-permute-start(f32[1,2048]{1,0:T(1,128)S(1)} %gain.1), channel_id=1, source_target_pairs={{0,1},{1,0},{2,3},{3,2},{4,5},{5,4},{6,7},{7,6},{8,9},{9,8},{10,11... | collective-permute-start | bytes 24584 | tf_op jit(solution)/shard_map/ppermute | solution.py:222
  99.3 4.7 %collective-permute-done = f32[1,2048]{1,0:T(1,128)S(1)} collective-permute-done((f32[1,2048]{1,0:T(1,128)S(1)}, f32[1,2048]{1,0:T(1,128)S(1)}, u32[]{:S(2)}, u32[]{:S(2)}) %collective-permute-start) | collective-permute-done | bytes 8224 | tf_op jit(solution)/shard_map/ppermute | solution.py:222
  104.0 7.7 %collective-permute-start.2 = (f32[1,2048]{1,0:T(1,128)S(1)}, f32[1,2048]{1,0:T(1,128)S(1)}, u32[]{:S(2)}, u32[]{:S(2)}) collective-permute-start(f32[1,2048]{1,0:T(1,128)S(1)} %add.7.after_ref), channel_id=1, source_target_pairs={{0,256},{8,264},{16,272},{24,280},{32,288},{40,296},{48,304},{56,3... | collective-permute-start | bytes 24584 | tf_op jit(solution)/shard_map/ppermute | solution.py:223
  111.7 0.8 keep.1.keep_ref
  112.5 0.0 collective-permute-done.1.arrived_ref
  112.5 1.8 %add.9 = bf16[1,1024,256]{2,1,0:T(8,128)(2,1)} custom-call(f32[1024,256]{1,0:T(8,128)S(1)} %keep.1.keep_ref, bf16[1024,256]{1,0:T(8,128)(2,1)} %collective-permute-done.1.arrived_ref), custom_call_target="tpu_custom_call" | custom-call | bytes 1048576 | tf_op jit(solution)/shard_map/add/pallas_call | solution.py:233
  114.4 0.3 collective-permute-done.2
  114.7 0.6 add.8
  (1 shorter events, 0.0 us)
Async XLA Ops:
  3.9 70.5 %copy-start = (bf16[8,128,256]{2,1,0:T(8,128)(2,1)}, bf16[8,128,256]{2,1,0:T(8,128)(2,1)S(1)}, u32[]{:S(2)}) copy-start(bf16[8,128,256]{2,1,0:T(8,128)(2,1)S(1)} %get-tuple-element.12) | copy-start | bytes 1572868
  3.9 74.2 %copy-start.1 = (f32[1,2048]{1,0:T(1,128)S(1)}, f32[1,2048]{1,0:T(1,128)}, u32[]{:S(2)}) copy-start(f32[1,2048]{1,0:T(1,128)} %gain_ref.3) | copy-start | bytes 24580
  74.4 18.8 %all-to-all-start.1 = ((bf16[8,128,256]{2,1,0:T(8,128)(2,1)}), bf16[8,128,256]{2,1,0:T(8,128)(2,1)S(1)}, u32[]{:S(2)}, u32[]{:S(2)}) async-start(bf16[8,128,256]{2,1,0:T(8,128)(2,1)} %copy-done), calls=%async_computation.1 | async-start | bytes 1048576 | tf_op jit(solution)/shard_map/all_to_all | solution.py:189
  80.1 32.4 %collective-permute-start.1 = (bf16[1024,256]{1,0:T(8,128)(2,1)}, bf16[1024,256]{1,0:T(8,128)(2,1)}, u32[]{:S(2)}, u32[]{:S(2)}) collective-permute-start(bf16[1024,256]{1,0:T(8,128)(2,1)} %get-tuple-element.13), channel_id=1, source_target_pairs={{0,256},{8,264},{16,272},{24,280},{32,288},{40,296},{48,304},{56,3... | collective-permute-start | bytes 1572872 | tf_op jit(solution)/shard_map/ppermute | solution.py:211
  94.5 9.5 %collective-permute-start = (f32[1,2048]{1,0:T(1,128)S(1)}, f32[1,2048]{1,0:T(1,128)S(1)}, u32[]{:S(2)}, u32[]{:S(2)}) collective-permute-start(f32[1,2048]{1,0:T(1,128)S(1)} %gain.1), channel_id=1, source_target_pairs={{0,1},{1,0},{2,3},{3,2},{4,5},{5,4},{6,7},{7,6},{8,9},{9,8},{10,11... | collective-permute-start | bytes 24584 | tf_op jit(solution)/shard_map/ppermute | solution.py:222
  104.0 10.7 %collective-permute-start.2 = (f32[1,2048]{1,0:T(1,128)S(1)}, f32[1,2048]{1,0:T(1,128)S(1)}, u32[]{:S(2)}, u32[]{:S(2)}) collective-permute-start(f32[1,2048]{1,0:T(1,128)S(1)} %add.7.after_ref), channel_id=1, source_target_pairs={{0,256},{8,264},{16,272},{24,280},{32,288},{40,296},{48,304},{56,3... | collective-permute-start | bytes 24584 | tf_op jit(solution)/shard_map/ppermute | solution.py:223

commit v4 on v3

--- a/solution.py
+++ b/solution.py
@@ -29,8 +29,7 @@
 
 
 def split_kernel(
-    order_ref, upper_ref, acts_ref, cot_ref, first_ref, second_ref,
-    acts_own, cot_own, keep_own, acts_sem, cot_sem, keep_sem,
+    order_ref, upper_ref, acts_ref, cot_ref, first_ref, second_ref, acts_own, cot_own, acts_sem, cot_sem
 ):
     groups = first_ref.shape[0]
     _, batches, tokens, width = acts_ref.shape
@@ -43,7 +42,6 @@
     load_cot.start()
     keep_at = pl.multiple_of(upper_ref[0] * half, 128)
     send_at = pl.multiple_of((1 - upper_ref[0]) * half, 128)
-    stores = []
     for m in range(batches):
         copies[m].wait()
         rows = slice(m * tokens, (m + 1) * tokens)
@@ -60,14 +58,9 @@
         send = (cot_own[slot, :, pl.ds(send_at, half)].astype(jnp.float32) * rstd).astype(jnp.bfloat16)
         keep = (cot_own[slot, :, pl.ds(keep_at, half)].astype(jnp.float32) * rstd).astype(jnp.bfloat16)
         for q in range(groups):
-            keep_own[q, rows, :] = keep
-        stores.append(pltpu.make_async_copy(keep_own.at[:, rows], second_ref.at[:, rows], keep_sem.at[m]))
-        stores[-1].start()
-        for q in range(groups):
+            second_ref[q, rows, :] = keep
             first_ref[q, rows, :half] = send
             first_ref[q, rows, half:] = acts_own[m, :, q * slab : (q + 1) * slab]
-    for store in stores:
-        store.wait()
 
 
 def split(acts, cotangent, order, upper, groups):
@@ -80,14 +73,12 @@
         split_kernel,
         out_shape=tuple(jax.ShapeDtypeStruct((groups, batches * tokens, n), jnp.bfloat16) for n in sizes),
         in_specs=[SMEM, SMEM, HBM, HBM],
-        out_specs=(VMEM, HBM),
+        out_specs=(VMEM, VMEM),
         scratch_shapes=[
             pltpu.VMEM((batches, tokens, width), jnp.bfloat16),
             pltpu.VMEM((batches, tokens, keys), jnp.bfloat16),
-            pltpu.VMEM((groups, batches * tokens, half), jnp.bfloat16),
             pltpu.SemaphoreType.DMA((batches,)),
             pltpu.SemaphoreType.DMA,
-            pltpu.SemaphoreType.DMA((batches,)),
         ],
         cost_estimate=cost(5 << 20),
         compiler_params=pltpu.CompilerParams(vmem_limit_bytes=SPLIT << 18),
@@ -116,43 +107,34 @@
     return copy
 
 
-def send_kernel(upper_ref, replica_ref, block_ref, weight_ref, gain_ref, send_ref, gterm_ref, own_ref, total_ref, sem):
+def scaled_kernel(replica_ref, grads_ref, block_ref, gain_ref, out_ref):
+    rows, half = out_ref.shape
+    first = pl.multiple_of(replica_ref[0] * rows, rows)
+    grads = grads_ref[:, :half]
+    for at in range(0, rows, TILE):
+        gain = gain_ref[:, pl.ds(pl.multiple_of(first + at, 128), TILE)].reshape(TILE, 1)
+        out_ref[at : at + TILE, :] = (half_product(block_ref, grads, at, half) * gain).astype(out_ref.dtype)
+
+
+def gain_kernel(keeping, upper_ref, replica_ref, grads_ref, block_ref, weight_ref, *refs):
+    before, (gterm_ref, own_ref, total_ref, sem) = refs[:keeping], refs[keeping:]
     rows, half = own_ref.shape
     first = pl.multiple_of(replica_ref[0] * rows, rows)
-    fetch = fetch_weight(weight_ref, own_ref, sem, first, pl.multiple_of((1 - upper_ref[0]) * half, half))
-    grads = block_ref[:, :half]
-    for at in range(0, rows, TILE):
-        total = half_product(block_ref, grads, at, half)
-        gain = gain_ref[:, pl.ds(pl.multiple_of(first + at, 128), TILE)].reshape(TILE, 1)
-        send_ref[at : at + TILE, :] = (total * gain).astype(jnp.bfloat16)
-        total_ref[at : at + TILE, :] = total
-    fetch.wait()
-    for at in range(0, rows, TILE):
-        gterm_ref[:, at : at + TILE] = gain_terms(total_ref[at : at + TILE, :], own_ref[at : at + TILE, :])
-
-
-def gain_kernel(upper_ref, replica_ref, before_ref, grads_ref, block_ref, weight_ref, gterm_ref, own_ref, total_ref, sem):
-    rows, half = own_ref.shape
-    first = pl.multiple_of(replica_ref[0] * rows, rows)
-    fetch = fetch_weight(weight_ref, own_ref, sem, first, pl.multiple_of(upper_ref[0] * half, half))
-    gterm_ref[...] = jnp.zeros_like(gterm_ref)
-    grads = grads_ref[...]
+    side = upper_ref[0] if keeping else 1 - upper_ref[0]
+    fetch = fetch_weight(weight_ref, own_ref, sem, first, pl.multiple_of(side * half, half))
+    if keeping:
+        gterm_ref[...] = jnp.zeros_like(gterm_ref)
+    grads = grads_ref[:, :half]
     for at in range(0, rows, TILE):
         total_ref[at : at + TILE, :] = half_product(block_ref, grads, at, half)
     fetch.wait()
     for at in range(0, rows, TILE):
         gterm = gain_terms(total_ref[at : at + TILE, :], own_ref[at : at + TILE, :])
-        gterm_ref[:, pl.ds(pl.multiple_of(first + at, 128), TILE)] = gterm + before_ref[:, at : at + TILE]
-
-
-def keep_kernel(replica_ref, after_ref, grads_ref, block_ref, gain_ref, keep_ref):
-    del after_ref
-    rows, half = keep_ref.shape
-    first = pl.multiple_of(replica_ref[0] * rows, rows)
-    grads = grads_ref[...]
-    for at in range(0, rows, TILE):
-        gain = gain_ref[:, pl.ds(pl.multiple_of(first + at, 128), TILE)].reshape(TILE, 1)
-        keep_ref[at : at + TILE, :] = half_product(block_ref, grads, at, half) * gain
+        if keeping:
+            where = pl.ds(pl.multiple_of(first + at, 128), TILE)
+            gterm_ref[:, where] = gterm + before[0][:, at : at + TILE]
+        else:
+            gterm_ref[:, at : at + TILE] = gterm
 
 
 def add_kernel(keep_ref, arrived_ref, out_ref, arrived_own, out_own, load_sem, store_sem):
@@ -198,38 +180,36 @@
         pltpu.VMEM((slab, half), jnp.float32),
         pltpu.SemaphoreType.DMA,
     ]
-    send, gterm = pl.pallas_call(
-        send_kernel,
-        out_shape=(jax.ShapeDtypeStruct((slab, half), jnp.bfloat16), jax.ShapeDtypeStruct((1, slab), jnp.float32)),
-        in_specs=[SMEM, SMEM, VMEM, HBM, VMEM],
-        out_specs=(VMEM, VMEM),
-        scratch_shapes=scratch,
-        cost_estimate=cost(),
-        compiler_params=params(),
-        name="send",
-    )(upper, replica, block, key_weight, gain)
-    arrived = lax.ppermute(send, "pipe", across)
-    gown = pl.pallas_call(
-        gain_kernel,
-        out_shape=jax.ShapeDtypeStruct(gain.shape, jnp.float32),
-        in_specs=[SMEM, SMEM, VMEM, VMEM, VMEM, HBM],
-        out_specs=VMEM,
-        scratch_shapes=scratch,
-        cost_estimate=cost(),
-        compiler_params=params(),
-        name="gain",
-    )(upper, replica, gterm, grads, block, key_weight)
-    gboth = gown + lax.ppermute(gown, "dp", [(0, 1), (1, 0)])
+
+    def scaled(grads, kind, name):
+        return pl.pallas_call(
+            scaled_kernel,
+            out_shape=jax.ShapeDtypeStruct((slab, half), kind),
+            in_specs=[SMEM, VMEM, VMEM, VMEM],
+            out_specs=VMEM,
+            cost_estimate=cost(),
+            compiler_params=params(),
+            name=name,
+        )(replica, grads, block, gain)
+
+    def gain_part(grads, *before):
+        return pl.pallas_call(
+            functools.partial(gain_kernel, len(before)),
+            out_shape=jax.ShapeDtypeStruct(gain.shape if before else (1, slab), jnp.float32),
+            in_specs=[SMEM, SMEM, VMEM, VMEM, HBM] + [VMEM] * len(before),
+            out_specs=VMEM,
+            scratch_shapes=scratch,
+            cost_estimate=cost(),
+            compiler_params=params(),
+            name="gain",
+        )(upper, replica, grads, block, key_weight, *before)
+
+    arrived = lax.ppermute(scaled(block, jnp.bfloat16, "send"), "pipe", across)
+    gown = gain_part(grads, gain_part(block))
+    gboth = lax.psum(gown, "dp")
     there = lax.ppermute(gboth, "pipe", across)
-    keep = pl.pallas_call(
-        keep_kernel,
-        out_shape=jax.ShapeDtypeStruct((slab, half), jnp.float32),
-        in_specs=[SMEM, pl.BlockSpec(memory_space=pl.ANY), VMEM, VMEM, VMEM],
-        out_specs=VMEM,
-        cost_estimate=cost(),
-        compiler_params=params(),
-        name="keep",
-    )(replica, gboth, grads, block, gain)
+    late_grads, _ = lax.optimization_barrier((grads, gboth))
+    keep = scaled(late_grads, jnp.float32, "keep")
     weight_out = pl.pallas_call(
         add_kernel,
         out_shape=jax.ShapeDtypeStruct((1, slab, half), jnp.bfloat16),

time: 116 us -> 115 us (level)
  blocking collectives: 70.5 us -> 79.4 us
  waiting for transfers between devices: 10.4 us -> 4.97 us
  starting transfers between devices: 23.9 us -> 19.1 us
    psum x0 -> x1, blocking collectives: none -> 8.92 us  [local(): gboth = lax.psum(gown, 'dp')]
    ppermute x2 -> x1, starting transfers between devices: 12.5 us -> 7.72 us  [local(): arrived = lax.ppermute(scaled(block, jnp.bfloat16, 'send'), 'pipe', across)]
    ppermute x2 -> x1, waiting for transfers between devices: 4.66 us -> 0.01 us  [local(): arrived = lax.ppermute(scaled(block, jnp.bfloat16, 'send'), 'pipe', across)]
    pallas_call x3 -> x4, Pallas kernels: 4.09 us -> 4.9 us  [the longest x2 2.57 us: gain_part(): pl.pallas_call(functools.partial(gain_kernel, len(before)), out_shape=jax...]
  transfers between devices with their start and end apart: 4 -> 3, of which waited for: 3 -> 2; matrix products, arithmetic and copies ran while one was open for 0% -> 0% of each run, Pallas kernels for 3% -> 5%
where the time goes in v4:
time: 115 us
  blocking collectives  79.4 us (69%)
  starting transfers between devices  19.1 us (17%)
  Pallas kernels  9.73 us (8%)
  waiting for transfers between devices  4.97 us (4%)
    all_to_all x1, blocking collectives, exchange(): lax.all_to_all(block, GROUP, 0, 0, tiled=True).reshape(groups * tokens, -1)  70.5 us
    psum x1, blocking collectives, local(): gboth = lax.psum(gown, 'dp')  8.92 us
    ppermute x1, starting transfers between devices, local(): arrived = lax.ppermute(scaled(block, jnp.bfloat16, 'send'), 'pipe', across)  7.72 us
    ppermute x1, starting transfers between devices, local(): there = lax.ppermute(gboth, 'pipe', across)  7.72 us
    all_to_all x1, waiting for transfers between devices, exchange(): lax.all_to_all(block, GROUP, 0, 0, tiled=True).reshape(groups * tokens, -1)  4.56 us
    all_to_all x1, starting transfers between devices, exchange(): lax.all_to_all(block, GROUP, 0, 0, tiled=True).reshape(groups * tokens, -1)  3.65 us
    pallas_call x1, Pallas kernels, split(): pl.pallas_call(split_kernel, out_shape=tuple((jax.ShapeDtypeStruct((group...  2.98 us
    pallas_call x2, Pallas kernels, gain_part(): pl.pallas_call(functools.partial(gain_kernel, len(before)), out_shape=jax...  2.57 us
  transfers between devices with their start and end apart: 3, of which 2 were waited for; matrix products, arithmetic and copies ran while one was open for 0% of the time, Pallas kernels for 5%

profile of v4, /device:TPU:70, one launch (start us, length us, event | category | flops | bytes accessed | tf_op | source)
XLA Modules:
  0.0 114.6 jit_solution(14674578004328617102)
XLA Ops:
  0.6 3.0 %split.1 = (bf16[8,128,1280]{2,1,0:T(8,128)(2,1)S(1)}, bf16[8,128,256]{2,1,0:T(8,128)(2,1)S(1)}) custom-call(s32[1,1,4]{2,1,0:T(1,128)} %order_ref.1, s32[1]{0:T(128)} %bitcast.1.upper_ref, bf16[1,4,32,8192]{3,2,1,0:T(8,128)(2,1)} %acts_ref.1, bf16[1,4,32,512]{3,2,1,0:T(8,128)(2,1)} %cot_ref.1), custom_call_target="tpu_custom_call" | custom-call | bytes 5242880 | tf_op jit(solution)/shard_map/split/pallas_call | solution.py:72
  3.6 0.0 copy-start
  3.6 0.0 copy-start.1
  3.7 70.5 %all_to_all.10 = bf16[8,128,1280]{2,1,0:T(8,128)(2,1)S(1)} all-to-all(bf16[8,128,1280]{2,1,0:T(8,128)(2,1)S(1)} %get-tuple-element.8), channel_id=1, replica_groups=mesh['pipe'=64,'fsdp'=4,'dp'=2] {'fsdp','dp'}, dimensions={0} | all-to-all | bytes 5242880 | tf_op jit(solution)/shard_map/all_to_all | solution.py:171
  74.2 0.0 copy-done
  74.2 3.7 %all-to-all-start.1 = ((bf16[8,128,256]{2,1,0:T(8,128)(2,1)}), bf16[8,128,256]{2,1,0:T(8,128)(2,1)S(1)}, u32[]{:S(2)}, u32[]{:S(2)}) async-start(bf16[8,128,256]{2,1,0:T(8,128)(2,1)} %copy-done), calls=%async_computation.1 | async-start | bytes 1048576 | tf_op jit(solution)/shard_map/all_to_all | solution.py:171
  77.8 0.0 copy-done.1
  77.8 1.6 %send.1 = bf16[1024,256]{1,0:T(8,128)(2,1)} custom-call(s32[1]{0:T(128)} %bitcast.replica_ref, bf16[1024,1280]{1,0:T(8,128)(2,1)S(1)} %bitcast.4, bf16[1024,1280]{1,0:T(8,128)(2,1)S(1)} %bitcast.5, f32[1,2048]{1,0:T(1,128)S(1)} %copy-done.1), custom_call_target="tpu_custom_call" | custom-call | tf_op jit(solution)/shard_map/send/pallas_call | solution.py:185
  79.4 7.7 %collective-permute-start = (bf16[1024,256]{1,0:T(8,128)(2,1)}, bf16[1024,256]{1,0:T(8,128)(2,1)}, u32[]{:S(2)}, u32[]{:S(2)}) collective-permute-start(bf16[1024,256]{1,0:T(8,128)(2,1)} %send.1), channel_id=1, source_target_pairs={{0,256},{8,264},{16,272},{24,280},{32,288},{40,296},{48,304},{56,3... | collective-permute-start | bytes 1572872 | tf_op jit(solution)/shard_map/ppermute | solution.py:207
  87.1 1.3 %gain.2.refs_0_ = f32[1,1024]{1,0:T(1,128)S(1)} custom-call(s32[1]{0:T(128)} %bitcast.1.upper_ref, s32[1]{0:T(128)} %bitcast.replica_ref, bf16[1024,1280]{1,0:T(8,128)(2,1)S(1)} %bitcast.6, bf16[1024,1280]{1,0:T(8,128)(2,1)S(1)} %bitcast.7, bf16[1,2048,512]{2,1,0:T(8,128)(2,1)} %weight_ref.3), custom_call_target="tpu_custom_call" | custom-call | tf_op jit(solution)/shard_map/gain/pallas_call | solution.py:196
  88.4 4.6 %all-to-all-done.1 = bf16[8,128,256]{2,1,0:T(8,128)(2,1)S(1)} async-done(((bf16[8,128,256]{2,1,0:T(8,128)(2,1)}), bf16[8,128,256]{2,1,0:T(8,128)(2,1)S(1)}, u32[]{:S(2)}, u32[]{:S(2)}) %all-to-all-start.1) | async-done | bytes 524320 | tf_op jit(solution)/shard_map/all_to_all | solution.py:171
  93.0 1.3 %gain.3 = f32[1,2048]{1,0:T(1,128)S(1)} custom-call(s32[1]{0:T(128)} %bitcast.1.upper_ref, s32[1]{0:T(128)} %bitcast.replica_ref, bf16[1024,256]{1,0:T(8,128)(2,1)S(1)} %bitcast.10, bf16[1024,1280]{1,0:T(8,128)(2,1)S(1)} %bitcast.8, bf16[1,2048,512]{2,1,0:T(8,128)(2,1)} %weight_ref.3, f32[1,1024]{1,0:T(1,128)S(1)} %gain.2.refs_0_), custom_call_target="tpu_custom_call" | custom-call | tf_op jit(solution)/shard_map/gain/pallas_call | solution.py:196
  94.3 8.9 %psum.7 = f32[1,2048]{1,0:T(1,128)S(1)} all-reduce(f32[1,2048]{1,0:T(1,128)S(1)} %gain.3), channel_id=1, replica_groups=mesh['pipe'=64,'fsdp'=4,'dp'=2] {'dp'}, use_global_device_ids=true, to_apply=%region_0.0 | all-reduce | flops 2048 | bytes 16384 | tf_op jit(solution)/shard_map/psum | solution.py:209
  103.2 7.7 %collective-permute-start.1 = (f32[1,2048]{1,0:T(1,128)S(1)}, f32[1,2048]{1,0:T(1,128)S(1)}, u32[]{:S(2)}, u32[]{:S(2)}) collective-permute-start(f32[1,2048]{1,0:T(1,128)S(1)} %psum.7), channel_id=1, source_target_pairs={{0,256},{8,264},{16,272},{24,280},{32,288},{40,296},{48,304},{56,3... | collective-permute-start | bytes 24584 | tf_op jit(solution)/shard_map/ppermute | solution.py:210
  110.9 0.8 keep.1.keep_ref
  111.7 0.0 collective-permute-done.arrived_ref
  111.7 1.8 %add.7 = bf16[1,1024,256]{2,1,0:T(8,128)(2,1)} custom-call(f32[1024,256]{1,0:T(8,128)S(1)} %keep.1.keep_ref, bf16[1024,256]{1,0:T(8,128)(2,1)} %collective-permute-done.arrived_ref), custom_call_target="tpu_custom_call" | custom-call | bytes 1048576 | tf_op jit(solution)/shard_map/add/pallas_call | solution.py:213
  113.6 0.4 collective-permute-done.1
  114.0 0.6 add.6
Async XLA Ops:
  3.6 70.5 %copy-start = (bf16[8,128,256]{2,1,0:T(8,128)(2,1)}, bf16[8,128,256]{2,1,0:T(8,128)(2,1)S(1)}, u32[]{:S(2)}) copy-start(bf16[8,128,256]{2,1,0:T(8,128)(2,1)S(1)} %get-tuple-element.9) | copy-start | bytes 1572868
  3.6 74.2 %copy-start.1 = (f32[1,2048]{1,0:T(1,128)S(1)}, f32[1,2048]{1,0:T(1,128)}, u32[]{:S(2)}) copy-start(f32[1,2048]{1,0:T(1,128)} %gain_ref.3) | copy-start | bytes 24580
  74.2 18.8 %all-to-all-start.1 = ((bf16[8,128,256]{2,1,0:T(8,128)(2,1)}), bf16[8,128,256]{2,1,0:T(8,128)(2,1)S(1)}, u32[]{:S(2)}, u32[]{:S(2)}) async-start(bf16[8,128,256]{2,1,0:T(8,128)(2,1)} %copy-done), calls=%async_computation.1 | async-start | bytes 1048576 | tf_op jit(solution)/shard_map/all_to_all | solution.py:171
  79.4 32.3 %collective-permute-start = (bf16[1024,256]{1,0:T(8,128)(2,1)}, bf16[1024,256]{1,0:T(8,128)(2,1)}, u32[]{:S(2)}, u32[]{:S(2)}) collective-permute-start(bf16[1024,256]{1,0:T(8,128)(2,1)} %send.1), channel_id=1, source_target_pairs={{0,256},{8,264},{16,272},{24,280},{32,288},{40,296},{48,304},{56,3... | collective-permute-start | bytes 1572872 | tf_op jit(solution)/shard_map/ppermute | solution.py:207
  103.2 10.8 %collective-permute-start.1 = (f32[1,2048]{1,0:T(1,128)S(1)}, f32[1,2048]{1,0:T(1,128)S(1)}, u32[]{:S(2)}, u32[]{:S(2)}) collective-permute-start(f32[1,2048]{1,0:T(1,128)S(1)} %psum.7), channel_id=1, source_target_pairs={{0,256},{8,264},{16,272},{24,280},{32,288},{40,296},{48,304},{56,3... | collective-permute-start | bytes 24584 | tf_op jit(solution)/shard_map/ppermute | solution.py:210

commit v5 on v4

--- a/solution.py
+++ b/solution.py
@@ -9,6 +9,7 @@
 
 GROUP = ("fsdp", "dp")
 TILE = 256
+BAND = 128
 SPLIT = 80
 STEPS = 4
 EPS = 1e-05
@@ -116,6 +117,24 @@
         out_ref[at : at + TILE, :] = (half_product(block_ref, grads, at, half) * gain).astype(out_ref.dtype)
 
 
+def send_kernel(replica_ref, block_ref, gain_ref, out_ref, own_ref, sem):
+    rows, half = out_ref.shape
+    first = pl.multiple_of(replica_ref[0] * rows, rows)
+    grads = block_ref[:, :half]
+    stores = []
+    for at in range(0, rows, BAND):
+        band = pl.ds(at, BAND)
+        gain = gain_ref[:, pl.ds(pl.multiple_of(first + at, 128), BAND)].reshape(BAND, 1)
+        total = lax.dot_general(
+            block_ref[:, half + at : half + at + BAND], grads, (((0,), (0,)), ((), ())), preferred_element_type=jnp.float32
+        )
+        own_ref[band, :] = (total * gain).astype(out_ref.dtype)
+        stores.append(pltpu.make_async_copy(own_ref.at[band], out_ref.at[band], sem.at[at // BAND]))
+        stores[-1].start()
+    for store in stores:
+        store.wait()
+
+
 def gain_kernel(keeping, upper_ref, replica_ref, grads_ref, block_ref, weight_ref, *refs):
     before, (gterm_ref, own_ref, total_ref, sem) = refs[:keeping], refs[keeping:]
     rows, half = own_ref.shape
@@ -204,27 +223,23 @@
             name="gain",
         )(upper, replica, grads, block, key_weight, *before)
 
-    arrived = lax.ppermute(scaled(block, jnp.bfloat16, "send"), "pipe", across)
+    send = pl.pallas_call(
+        send_kernel,
+        out_shape=jax.ShapeDtypeStruct((slab, half), jnp.bfloat16),
+        in_specs=[SMEM, VMEM, VMEM],
+        out_specs=HBM,
+        scratch_shapes=[pltpu.VMEM((slab, half), jnp.bfloat16), pltpu.SemaphoreType.DMA((slab // BAND,))],
+        cost_estimate=cost(),
+        compiler_params=params(),
+        name="send",
+    )(replica, block, gain)
+    arrived = lax.ppermute(send, "pipe", across)
     gown = gain_part(grads, gain_part(block))
     gboth = lax.psum(gown, "dp")
     there = lax.ppermute(gboth, "pipe", across)
     late_grads, _ = lax.optimization_barrier((grads, gboth))
     keep = scaled(late_grads, jnp.float32, "keep")
-    weight_out = pl.pallas_call(
-        add_kernel,
-        out_shape=jax.ShapeDtypeStruct((1, slab, half), jnp.bfloat16),
-        in_specs=[VMEM, ARRIVED],
-        out_specs=HBM,
-        scratch_shapes=[
-            pltpu.VMEM((slab, half), jnp.bfloat16),
-            pltpu.VMEM((slab, half), jnp.bfloat16),
-            pltpu.SemaphoreType.DMA((STEPS,)),
-            pltpu.SemaphoreType.DMA((STEPS,)),
-        ],
-        cost_estimate=cost(ADDCOST),
-        compiler_params=params(),
-        name="add",
-    )(keep, arrived)
+    weight_out = (keep + arrived.astype(jnp.float32)).astype(jnp.bfloat16)[None]
     return (weight_out, gboth + there)
 
 

time: 115 us -> 115 us (level)
  other arithmetic: 0.61 us -> 2.56 us
  Pallas kernels: 9.73 us -> 7.84 us
    broadcast_in_dim x0 -> x1, other arithmetic: none -> 1.95 us  [local(): weight_out = (keep + arrived.astype(jnp.float32)).astype(jnp.bfloat16)[None]]
    pallas_call x2 -> x1, Pallas kernels: 2.33 us -> 0.77 us  [scaled(): pl.pallas_call(scaled_kernel, out_shape=jax.ShapeDtypeStruct((slab, half)...]
  transfers between devices with their start and end apart: 3 -> 3, of which waited for: 2 -> 2; matrix products, arithmetic and copies ran while one was open for 0% -> 2% of each run, Pallas kernels for 5% -> 3%
where the time goes in v5:
time: 115 us
  blocking collectives  79.4 us (69%)
  starting transfers between devices  19.1 us (17%)
  Pallas kernels  7.84 us (7%)
  waiting for transfers between devices  4.88 us (4%)
  other arithmetic  2.56 us (2%)
    all_to_all x1, blocking collectives, exchange(): lax.all_to_all(block, GROUP, 0, 0, tiled=True).reshape(groups * tokens, -1)  70.5 us
    psum x1, blocking collectives, local(): gboth = lax.psum(gown, 'dp')  8.92 us
    ppermute x1, starting transfers between devices, local(): arrived = lax.ppermute(send, 'pipe', across)  7.73 us
    ppermute x1, starting transfers between devices, local(): there = lax.ppermute(gboth, 'pipe', across)  7.72 us
    all_to_all x1, waiting for transfers between devices, exchange(): lax.all_to_all(block, GROUP, 0, 0, tiled=True).reshape(groups * tokens, -1)  4.58 us
    all_to_all x1, starting transfers between devices, exchange(): lax.all_to_all(block, GROUP, 0, 0, tiled=True).reshape(groups * tokens, -1)  3.65 us
    pallas_call x1, Pallas kernels, split(): pl.pallas_call(split_kernel, out_shape=tuple((jax.ShapeDtypeStruct((group...  2.98 us
    pallas_call x2, Pallas kernels, gain_part(): pl.pallas_call(functools.partial(gain_kernel, len(before)), out_shape=jax...  2.57 us
  transfers between devices with their start and end apart: 3, of which 2 were waited for; matrix products, arithmetic and copies ran while one was open for 2% of the time, Pallas kernels for 3%

profile of v5, /device:TPU:70, one launch (start us, length us, event | category | flops | bytes accessed | tf_op | source)
XLA Modules:
  0.0 114.5 jit_solution(3001869662522063770)
XLA Ops:
  0.6 3.0 %split.1 = (bf16[8,128,1280]{2,1,0:T(8,128)(2,1)S(1)}, bf16[8,128,256]{2,1,0:T(8,128)(2,1)S(1)}) custom-call(s32[1,1,4]{2,1,0:T(1,128)} %order_ref.1, s32[1]{0:T(128)} %bitcast.1.upper_ref, bf16[1,4,32,8192]{3,2,1,0:T(8,128)(2,1)} %acts_ref.1, bf16[1,4,32,512]{3,2,1,0:T(8,128)(2,1)} %cot_ref.1), custom_call_target="tpu_custom_call" | custom-call | bytes 5242880 | tf_op jit(solution)/shard_map/split/pallas_call | solution.py:73
  3.6 0.0 copy-start
  3.6 0.0 copy-start.1
  3.7 70.5 %all_to_all.10 = bf16[8,128,1280]{2,1,0:T(8,128)(2,1)S(1)} all-to-all(bf16[8,128,1280]{2,1,0:T(8,128)(2,1)S(1)} %get-tuple-element.8), channel_id=1, replica_groups=mesh['pipe'=64,'fsdp'=4,'dp'=2] {'fsdp','dp'}, dimensions={0} | all-to-all | bytes 5242880 | tf_op jit(solution)/shard_map/all_to_all | solution.py:190
  74.2 0.0 copy-done
  74.2 3.7 %all-to-all-start.1 = ((bf16[8,128,256]{2,1,0:T(8,128)(2,1)}), bf16[8,128,256]{2,1,0:T(8,128)(2,1)S(1)}, u32[]{:S(2)}, u32[]{:S(2)}) async-start(bf16[8,128,256]{2,1,0:T(8,128)(2,1)} %copy-done), calls=%async_computation.1 | async-start | bytes 1048576 | tf_op jit(solution)/shard_map/all_to_all | solution.py:190
  77.8 0.0 copy-done.1
  77.8 1.5 %send.1 = bf16[1024,256]{1,0:T(8,128)(2,1)} custom-call(s32[1]{0:T(128)} %bitcast.replica_ref, bf16[1024,1280]{1,0:T(8,128)(2,1)S(1)} %bitcast.6, f32[1,2048]{1,0:T(1,128)S(1)} %copy-done.1), custom_call_target="tpu_custom_call" | custom-call | tf_op jit(solution)/shard_map/send/pallas_call | solution.py:226
  79.4 7.7 %collective-permute-start = (bf16[1024,256]{1,0:T(8,128)(2,1)}, bf16[1024,256]{1,0:T(8,128)(2,1)}, u32[]{:S(2)}, u32[]{:S(2)}) collective-permute-start(bf16[1024,256]{1,0:T(8,128)(2,1)} %send.1), channel_id=1, source_target_pairs={{0,256},{8,264},{16,272},{24,280},{32,288},{40,296},{48,304},{56,3... | collective-permute-start | bytes 1572872 | tf_op jit(solution)/shard_map/ppermute | solution.py:236
  87.1 1.3 %gain.2.refs_0_ = f32[1,1024]{1,0:T(1,128)S(1)} custom-call(s32[1]{0:T(128)} %bitcast.1.upper_ref, s32[1]{0:T(128)} %bitcast.replica_ref, bf16[1024,1280]{1,0:T(8,128)(2,1)S(1)} %bitcast.7, bf16[1024,1280]{1,0:T(8,128)(2,1)S(1)} %bitcast.8, bf16[1,2048,512]{2,1,0:T(8,128)(2,1)} %weight_ref.3), custom_call_target="tpu_custom_call" | custom-call | tf_op jit(solution)/shard_map/gain/pallas_call | solution.py:215
  88.4 4.6 %all-to-all-done.1 = bf16[8,128,256]{2,1,0:T(8,128)(2,1)S(1)} async-done(((bf16[8,128,256]{2,1,0:T(8,128)(2,1)}), bf16[8,128,256]{2,1,0:T(8,128)(2,1)S(1)}, u32[]{:S(2)}, u32[]{:S(2)}) %all-to-all-start.1) | async-done | bytes 524320 | tf_op jit(solution)/shard_map/all_to_all | solution.py:190
  93.0 1.3 %gain.3 = f32[1,2048]{1,0:T(1,128)S(1)} custom-call(s32[1]{0:T(128)} %bitcast.1.upper_ref, s32[1]{0:T(128)} %bitcast.replica_ref, bf16[1024,256]{1,0:T(8,128)(2,1)S(1)} %bitcast.11, bf16[1024,1280]{1,0:T(8,128)(2,1)S(1)} %bitcast.9, bf16[1,2048,512]{2,1,0:T(8,128)(2,1)} %weight_ref.3, f32[1,1024]{1,0:T(1,128)S(1)} %gain.2.refs_0_), custom_call_target="tpu_custom_call" | custom-call | tf_op jit(solution)/shard_map/gain/pallas_call | solution.py:215
  94.3 8.9 %psum.7 = f32[1,2048]{1,0:T(1,128)S(1)} all-reduce(f32[1,2048]{1,0:T(1,128)S(1)} %gain.3), channel_id=1, replica_groups=mesh['pipe'=64,'fsdp'=4,'dp'=2] {'dp'}, use_global_device_ids=true, to_apply=%region_0.0 | all-reduce | flops 2048 | bytes 16384 | tf_op jit(solution)/shard_map/psum | solution.py:238
  103.2 7.7 %collective-permute-start.1 = (f32[1,2048]{1,0:T(1,128)S(1)}, f32[1,2048]{1,0:T(1,128)S(1)}, u32[]{:S(2)}, u32[]{:S(2)}) collective-permute-start(f32[1,2048]{1,0:T(1,128)S(1)} %psum.7), channel_id=1, source_target_pairs={{0,256},{8,264},{16,272},{24,280},{32,288},{40,296},{48,304},{56,3... | collective-permute-start | bytes 24584 | tf_op jit(solution)/shard_map/ppermute | solution.py:239
  110.9 0.8 keep.1
  111.7 0.0 collective-permute-done
  111.7 1.9 %fusion = bf16[1,1024,256]{2,1,0:T(8,128)(2,1)} fusion(f32[1024,256]{1,0:T(8,128)S(1)} %keep.1, bf16[1024,256]{1,0:T(8,128)(2,1)} %collective-permute-done), kind=kLoop, calls=%fused_computation.1 | loop fusion | flops 786432 | bytes 2097152 | tf_op jit(solution)/shard_map/broadcast_in_dim | solution.py:242
  113.7 0.3 collective-permute-done.1
  113.9 0.6 add.9
Async XLA Ops:
  3.6 70.5 %copy-start = (bf16[8,128,256]{2,1,0:T(8,128)(2,1)}, bf16[8,128,256]{2,1,0:T(8,128)(2,1)S(1)}, u32[]{:S(2)}) copy-start(bf16[8,128,256]{2,1,0:T(8,128)(2,1)S(1)} %get-tuple-element.9) | copy-start | bytes 1572868
  3.6 74.2 %copy-start.1 = (f32[1,2048]{1,0:T(1,128)S(1)}, f32[1,2048]{1,0:T(1,128)}, u32[]{:S(2)}) copy-start(f32[1,2048]{1,0:T(1,128)} %gain_ref.3) | copy-start | bytes 24580
  74.2 18.8 %all-to-all-start.1 = ((bf16[8,128,256]{2,1,0:T(8,128)(2,1)}), bf16[8,128,256]{2,1,0:T(8,128)(2,1)S(1)}, u32[]{:S(2)}, u32[]{:S(2)}) async-start(bf16[8,128,256]{2,1,0:T(8,128)(2,1)} %copy-done), calls=%async_computation.1 | async-start | bytes 1048576 | tf_op jit(solution)/shard_map/all_to_all | solution.py:190
  79.4 32.3 %collective-permute-start = (bf16[1024,256]{1,0:T(8,128)(2,1)}, bf16[1024,256]{1,0:T(8,128)(2,1)}, u32[]{:S(2)}, u32[]{:S(2)}) collective-permute-start(bf16[1024,256]{1,0:T(8,128)(2,1)} %send.1), channel_id=1, source_target_pairs={{0,256},{8,264},{16,272},{24,280},{32,288},{40,296},{48,304},{56,3... | collective-permute-start | bytes 1572872 | tf_op jit(solution)/shard_map/ppermute | solution.py:236
  103.2 10.8 %collective-permute-start.1 = (f32[1,2048]{1,0:T(1,128)S(1)}, f32[1,2048]{1,0:T(1,128)S(1)}, u32[]{:S(2)}, u32[]{:S(2)}) collective-permute-start(f32[1,2048]{1,0:T(1,128)S(1)} %psum.7), channel_id=1, source_target_pairs={{0,256},{8,264},{16,272},{24,280},{32,288},{40,296},{48,304},{56,3... | collective-permute-start | bytes 24584 | tf_op jit(solution)/shard_map/ppermute | solution.py:239

commit v6 on v5

--- a/solution.py
+++ b/solution.py
@@ -235,10 +235,11 @@
     )(replica, block, gain)
     arrived = lax.ppermute(send, "pipe", across)
     gown = gain_part(grads, gain_part(block))
-    gboth = lax.psum(gown, "dp")
+    gboth = gown + lax.ppermute(gown, "dp", [(0, 1), (1, 0)])
+    late_grads, _ = lax.optimization_barrier((grads, gown))
+    keep = scaled(late_grads, jnp.float32, "keep")
+    gboth, keep = lax.optimization_barrier((gboth, keep))
     there = lax.ppermute(gboth, "pipe", across)
-    late_grads, _ = lax.optimization_barrier((grads, gboth))
-    keep = scaled(late_grads, jnp.float32, "keep")
     weight_out = (keep + arrived.astype(jnp.float32)).astype(jnp.bfloat16)[None]
     return (weight_out, gboth + there)
 

time: 115 us -> 115 us (level)
  blocking collectives: 79.4 us -> 70.5 us
  starting transfers between devices: 19.1 us -> 23.9 us
  waiting for transfers between devices: 4.88 us -> 8.98 us
    psum x1 -> x0, blocking collectives: 8.92 us -> none  [local(): gboth = lax.psum(gown, 'dp')]
    ppermute x0 -> x1, starting transfers between devices: none -> 4.79 us  [local(): gboth = gown + lax.ppermute(gown, 'dp', [(0, 1), (1, 0)])]
    ppermute x0 -> x1, waiting for transfers between devices: none -> 3.89 us  [local(): gboth = gown + lax.ppermute(gown, 'dp', [(0, 1), (1, 0)])]
  transfers between devices with their start and end apart: 3 -> 4, of which waited for: 2 -> 3; matrix products, arithmetic and copies ran while one was open for 2% -> 2% of each run, Pallas kernels for 3% -> 3%
where the time goes in v6:
time: 115 us
  blocking collectives  70.5 us (61%)
  starting transfers between devices  23.9 us (21%)
  waiting for transfers between devices  8.98 us (8%)
  Pallas kernels  7.83 us (7%)
  other arithmetic  2.57 us (2%)
    all_to_all x1, blocking collectives, exchange(): lax.all_to_all(block, GROUP, 0, 0, tiled=True).reshape(groups * tokens, -1)  70.5 us
    ppermute x1, starting transfers between devices, local(): arrived = lax.ppermute(send, 'pipe', across)  7.73 us
    ppermute x1, starting transfers between devices, local(): there = lax.ppermute(gboth, 'pipe', across)  7.73 us
    ppermute x1, starting transfers between devices, local(): gboth = gown + lax.ppermute(gown, 'dp', [(0, 1), (1, 0)])  4.79 us
    all_to_all x1, waiting for transfers between devices, exchange(): lax.all_to_all(block, GROUP, 0, 0, tiled=True).reshape(groups * tokens, -1)  4.59 us
    ppermute x1, waiting for transfers between devices, local(): gboth = gown + lax.ppermute(gown, 'dp', [(0, 1), (1, 0)])  3.89 us
    all_to_all x1, starting transfers between devices, exchange(): lax.all_to_all(block, GROUP, 0, 0, tiled=True).reshape(groups * tokens, -1)  3.65 us
    pallas_call x1, Pallas kernels, split(): pl.pallas_call(split_kernel, out_shape=tuple((jax.ShapeDtypeStruct((group...  2.98 us
  transfers between devices with their start and end apart: 4, of which 3 were waited for; matrix products, arithmetic and copies ran while one was open for 2% of the time, Pallas kernels for 3%

profile of v6, /device:TPU:70, one launch (start us, length us, event | category | flops | bytes accessed | tf_op | source)
XLA Modules:
  0.0 114.5 jit_solution(10593877259184021467)
XLA Ops:
  0.6 3.0 %split.1 = (bf16[8,128,1280]{2,1,0:T(8,128)(2,1)S(1)}, bf16[8,128,256]{2,1,0:T(8,128)(2,1)S(1)}) custom-call(s32[1,1,4]{2,1,0:T(1,128)} %order_ref.1, s32[1]{0:T(128)} %bitcast.upper_ref, bf16[1,4,32,8192]{3,2,1,0:T(8,128)(2,1)} %acts_ref.1, bf16[1,4,32,512]{3,2,1,0:T(8,128)(2,1)} %cot_ref.1), custom_call_target="tpu_custom_call" | custom-call | bytes 5242880 | tf_op jit(solution)/shard_map/split/pallas_call | solution.py:73
  3.6 0.0 copy-start
  3.6 0.0 copy-start.1
  3.7 70.5 %all_to_all.10 = bf16[8,128,1280]{2,1,0:T(8,128)(2,1)S(1)} all-to-all(bf16[8,128,1280]{2,1,0:T(8,128)(2,1)S(1)} %get-tuple-element.10), channel_id=1, replica_groups=mesh['pipe'=64,'fsdp'=4,'dp'=2] {'fsdp','dp'}, dimensions={0} | all-to-all | bytes 5242880 | tf_op jit(solution)/shard_map/all_to_all | solution.py:190
  74.2 0.0 copy-done
  74.2 3.7 %all-to-all-start.1 = ((bf16[8,128,256]{2,1,0:T(8,128)(2,1)}), bf16[8,128,256]{2,1,0:T(8,128)(2,1)S(1)}, u32[]{:S(2)}, u32[]{:S(2)}) async-start(bf16[8,128,256]{2,1,0:T(8,128)(2,1)} %copy-done), calls=%async_computation.1 | async-start | bytes 1048576 | tf_op jit(solution)/shard_map/all_to_all | solution.py:190
  77.8 0.0 copy-done.1
  77.8 1.5 %send.1 = bf16[1024,256]{1,0:T(8,128)(2,1)} custom-call(s32[1]{0:T(128)} %bitcast.1.replica_ref, bf16[1024,1280]{1,0:T(8,128)(2,1)S(1)} %bitcast.6, f32[1,2048]{1,0:T(1,128)S(1)} %copy-done.1), custom_call_target="tpu_custom_call" | custom-call | tf_op jit(solution)/shard_map/send/pallas_call | solution.py:226
  79.4 7.7 %collective-permute-start.1 = (bf16[1024,256]{1,0:T(8,128)(2,1)}, bf16[1024,256]{1,0:T(8,128)(2,1)}, u32[]{:S(2)}, u32[]{:S(2)}) collective-permute-start(bf16[1024,256]{1,0:T(8,128)(2,1)} %send.1), channel_id=1, source_target_pairs={{0,256},{8,264},{16,272},{24,280},{32,288},{40,296},{48,304},{56,3... | collective-permute-start | bytes 1572872 | tf_op jit(solution)/shard_map/ppermute | solution.py:236
  87.1 1.3 %gain.2.refs_0_ = f32[1,1024]{1,0:T(1,128)S(1)} custom-call(s32[1]{0:T(128)} %bitcast.upper_ref, s32[1]{0:T(128)} %bitcast.1.replica_ref, bf16[1024,1280]{1,0:T(8,128)(2,1)S(1)} %bitcast.7, bf16[1024,1280]{1,0:T(8,128)(2,1)S(1)} %bitcast.8, bf16[1,2048,512]{2,1,0:T(8,128)(2,1)} %weight_ref.3), custom_call_target="tpu_custom_call" | custom-call | tf_op jit(solution)/shard_map/gain/pallas_call | solution.py:215
  88.4 4.6 %all-to-all-done.1 = bf16[8,128,256]{2,1,0:T(8,128)(2,1)S(1)} async-done(((bf16[8,128,256]{2,1,0:T(8,128)(2,1)}), bf16[8,128,256]{2,1,0:T(8,128)(2,1)S(1)}, u32[]{:S(2)}, u32[]{:S(2)}) %all-to-all-start.1) | async-done | bytes 524320 | tf_op jit(solution)/shard_map/all_to_all | solution.py:190
  93.0 1.3 %gain.3 = f32[1,2048]{1,0:T(1,128)S(1)} custom-call(s32[1]{0:T(128)} %bitcast.upper_ref, s32[1]{0:T(128)} %bitcast.1.replica_ref, bf16[1024,256]{1,0:T(8,128)(2,1)S(1)} %bitcast.11, bf16[1024,1280]{1,0:T(8,128)(2,1)S(1)} %bitcast.9, bf16[1,2048,512]{2,1,0:T(8,128)(2,1)} %weight_ref.3, f32[1,1024]{1,0:T(1,128)S(1)} %gain.2.refs_0_), custom_call_target="tpu_custom_call" | custom-call | tf_op jit(solution)/shard_map/gain/pallas_call | solution.py:215
  94.3 4.8 %collective-permute-start = (f32[1,2048]{1,0:T(1,128)S(1)}, f32[1,2048]{1,0:T(1,128)S(1)}, u32[]{:S(2)}, u32[]{:S(2)}) collective-permute-start(f32[1,2048]{1,0:T(1,128)S(1)} %gain.3), channel_id=1, source_target_pairs={{0,1},{1,0},{2,3},{3,2},{4,5},{5,4},{6,7},{7,6},{8,9},{9,8},{10,11... | collective-permute-start | bytes 24584 | tf_op jit(solution)/shard_map/ppermute | solution.py:238
  99.1 0.8 keep.1
  99.8 3.9 %collective-permute-done = f32[1,2048]{1,0:T(1,128)S(1)} collective-permute-done((f32[1,2048]{1,0:T(1,128)S(1)}, f32[1,2048]{1,0:T(1,128)S(1)}, u32[]{:S(2)}, u32[]{:S(2)}) %collective-permute-start) | collective-permute-done | bytes 8224 | tf_op jit(solution)/shard_map/ppermute | solution.py:238
  103.7 7.7 %collective-permute-start.2 = (f32[1,2048]{1,0:T(1,128)S(1)}, f32[1,2048]{1,0:T(1,128)S(1)}, u32[]{:S(2)}, u32[]{:S(2)}) collective-permute-start(f32[1,2048]{1,0:T(1,128)S(1)} %add.9), channel_id=1, source_target_pairs={{0,256},{8,264},{16,272},{24,280},{32,288},{40,296},{48,304},{56,3... | collective-permute-start | bytes 24584 | tf_op jit(solution)/shard_map/ppermute | solution.py:242
  111.5 0.0 collective-permute-done.1
  111.5 1.9 %fusion = bf16[1,1024,256]{2,1,0:T(8,128)(2,1)} fusion(f32[1024,256]{1,0:T(8,128)S(1)} %keep.1, bf16[1024,256]{1,0:T(8,128)(2,1)} %collective-permute-done.1), kind=kLoop, calls=%fused_computation.1 | loop fusion | flops 786432 | bytes 2097152 | tf_op jit(solution)/shard_map/broadcast_in_dim | solution.py:243
  113.4 0.5 collective-permute-done.2
  113.9 0.6 add.11
  (1 shorter events, 0.0 us)
Async XLA Ops:
  3.6 70.5 %copy-start = (bf16[8,128,256]{2,1,0:T(8,128)(2,1)}, bf16[8,128,256]{2,1,0:T(8,128)(2,1)S(1)}, u32[]{:S(2)}) copy-start(bf16[8,128,256]{2,1,0:T(8,128)(2,1)S(1)} %get-tuple-element.11) | copy-start | bytes 1572868
  3.6 74.2 %copy-start.1 = (f32[1,2048]{1,0:T(1,128)S(1)}, f32[1,2048]{1,0:T(1,128)}, u32[]{:S(2)}) copy-start(f32[1,2048]{1,0:T(1,128)} %gain_ref.3) | copy-start | bytes 24580
  74.2 18.8 %all-to-all-start.1 = ((bf16[8,128,256]{2,1,0:T(8,128)(2,1)}), bf16[8,128,256]{2,1,0:T(8,128)(2,1)S(1)}, u32[]{:S(2)}, u32[]{:S(2)}) async-start(bf16[8,128,256]{2,1,0:T(8,128)(2,1)} %copy-done), calls=%async_computation.1 | async-start | bytes 1048576 | tf_op jit(solution)/shard_map/all_to_all | solution.py:190
  79.4 32.1 %collective-permute-start.1 = (bf16[1024,256]{1,0:T(8,128)(2,1)}, bf16[1024,256]{1,0:T(8,128)(2,1)}, u32[]{:S(2)}, u32[]{:S(2)}) collective-permute-start(bf16[1024,256]{1,0:T(8,128)(2,1)} %send.1), channel_id=1, source_target_pairs={{0,256},{8,264},{16,272},{24,280},{32,288},{40,296},{48,304},{56,3... | collective-permute-start | bytes 1572872 | tf_op jit(solution)/shard_map/ppermute | solution.py:236
  94.3 9.5 %collective-permute-start = (f32[1,2048]{1,0:T(1,128)S(1)}, f32[1,2048]{1,0:T(1,128)S(1)}, u32[]{:S(2)}, u32[]{:S(2)}) collective-permute-start(f32[1,2048]{1,0:T(1,128)S(1)} %gain.3), channel_id=1, source_target_pairs={{0,1},{1,0},{2,3},{3,2},{4,5},{5,4},{6,7},{7,6},{8,9},{9,8},{10,11... | collective-permute-start | bytes 24584 | tf_op jit(solution)/shard_map/ppermute | solution.py:238
  103.7 10.2 %collective-permute-start.2 = (f32[1,2048]{1,0:T(1,128)S(1)}, f32[1,2048]{1,0:T(1,128)S(1)}, u32[]{:S(2)}, u32[]{:S(2)}) collective-permute-start(f32[1,2048]{1,0:T(1,128)S(1)} %add.9), channel_id=1, source_target_pairs={{0,256},{8,264},{16,272},{24,280},{32,288},{40,296},{48,304},{56,3... | collective-permute-start | bytes 24584 | tf_op jit(solution)/shard_map/ppermute | solution.py:242
